TPU v7x, 256 devices: a whole 4x4x8 slice. The times are simulated.
256 devices in a mesh: segment: 4 (over y_lo, core), dp: 64 (over z, x, y_hi).
Axes of the slice: x: 4, y: 4 (y_hi: 2, y_lo: 2; y = y_hi * 2 + y_lo), z: 8, core: 2. Of those that a mesh axis runs over, the one named last changes fastest.
Arguments:
- images: bfloat16 [512, 256, 1024], P('dp'), may hold values from -6 to 6
- texts: bfloat16 [512, 64, 1536], P('dp'), may hold values from -6 to 6
- section_weights: bfloat16 [4, 21504, 128], P('segment'), may hold values from -0.15625 to 0.15625
- uniting_weights: bfloat16 [3584, 1024], P('dp'), may hold values from -0.125 to 0.125
- codebooks: float32 [64, 2, 256, 1024], P('dp'), may hold values from -3 to 3
- neg_bank: bfloat16 [64, 256, 1024], P('dp'), may hold values from -6 to 6
- item_cats: int32 [4, 128, 1], replicated, may hold values from 0 to 63; in each aligned block of 128 rows (0 to 127, 128 to 255, ..., all dimensions but the last counted through in order) at most 2 rows name the same one
- cat_slot: int32 [64], replicated, may hold values from 0 to 63, each once
- neg_index: int32 [4, 128, 128], replicated, may hold values from 0 to 255
Outputs:
- uniting_grad: float32 [3584, 1024], P('dp')
- codebook_grad: float32 [64, 2, 256, 1024], P('dp')
- owner_loss: float32 [64], P('dp')
Inputs may be any that keep to these rules, and one draw needn't show every extreme that they name: `item_cats`: within one row of 128 no category appears more than 2 times, and in some row some category appears exactly 2 times. `cat_slot`: A permutation: every category has its own slot; slot t lies with owner t.
All inputs are finite; a program needn't handle non-finite values.
Results may differ from a plain program's by a relative error of at most 0.028.
Values may be sent and summed in bfloat16 or wider, within the bound.
A program may use at most 128 MiB of HBM per device.

v0:
```python
import math

import jax
import jax.numpy as jnp
from jax import lax
from jax.sharding import PartitionSpec as P

HEAD_IMG = 64
HEAD_TXT = 128
CAP = 2


norm_eps = 1e-06
rope_theta = 1000000.0
contrast_temp = 0.1
beta_weight = 1.0
highest = lax.Precision.HIGHEST


def gelu_value(inputs_f):
    return 0.5 * inputs_f * (1.0 + lax.erf(inputs_f / math.sqrt(2.0)))


def gelu_slope(inputs_f):
    return 0.5 * (1.0 + lax.erf(inputs_f / math.sqrt(2.0))) + inputs_f * jnp.exp(
        -0.5 * inputs_f * inputs_f
    ) / math.sqrt(2.0 * math.pi)


def rotate_pairs(tensor, positions):
    half_dim = tensor.shape[-1] // 2
    exponents = jnp.arange(half_dim).astype(jnp.float32) * (2.0 / tensor.shape[-1])
    inverse_freq = jnp.exp(-math.log(rope_theta) * exponents)
    angles = positions[:, None] * inverse_freq[None, :]
    cosine = jnp.concatenate([jnp.cos(angles), jnp.cos(angles)], axis=-1)[:, None, :]
    sine = jnp.concatenate([jnp.sin(angles), jnp.sin(angles)], axis=-1)[:, None, :]
    rotated = jnp.concatenate([-tensor[..., half_dim:], tensor[..., :half_dim]], axis=-1)
    return tensor * cosine + rotated * sine


def softmax_rows(scores):
    scores = scores - jnp.max(scores, axis=-1, keepdims=True)
    exp_scores = jnp.exp(scores)
    return (exp_scores / jnp.sum(exp_scores, axis=-1, keepdims=True)).astype(jnp.bfloat16)


def image_attention(images, flat_slot):
    item_count, patch_count, model_width = images.shape
    half_width = model_width // 2
    head_count = half_width // HEAD_IMG
    qkv_size = model_width * 3 * half_width
    w_qkv = flat_slot[:qkv_size].reshape(model_width, 3 * half_width)
    w_out = flat_slot[qkv_size : qkv_size + half_width * model_width].reshape(
        half_width, model_width
    )
    float_tokens = images.astype(jnp.float32)
    centred = float_tokens - jnp.mean(float_tokens, axis=-1, keepdims=True)
    variance = jnp.mean(centred * centred, axis=-1, keepdims=True)
    normed = (centred * lax.rsqrt(variance + norm_eps)).astype(jnp.bfloat16)
    projections = jnp.einsum(
        "bpd,de->bpe", normed, w_qkv, preferred_element_type=jnp.float32
    ).astype(jnp.bfloat16)
    queries = projections[..., :half_width].reshape(item_count, patch_count, head_count, HEAD_IMG)
    key_rows = projections[..., half_width : 2 * half_width].reshape(
        item_count, patch_count, head_count, HEAD_IMG
    )
    value_rows = projections[..., 2 * half_width :].reshape(
        item_count, patch_count, head_count, HEAD_IMG
    )
    scores = jnp.einsum(
        "bqhc,bkhc->bhqk", queries, key_rows, preferred_element_type=jnp.float32
    ) / math.sqrt(HEAD_IMG)
    probabilities = softmax_rows(scores)
    attended = jnp.einsum(
        "bhqk,bkhc->bqhc", probabilities, value_rows, preferred_element_type=jnp.float32
    ).astype(jnp.bfloat16)
    attended = attended.reshape(item_count, patch_count, half_width)
    projected = jnp.einsum("bpc,cd->bpd", attended, w_out, preferred_element_type=jnp.float32)
    return jnp.mean(projected, axis=1)


def text_attention(texts, flat_slot):
    item_count, token_count, model_width = texts.shape
    half_width = model_width // 2
    head_count = half_width // HEAD_TXT
    inner_width = half_width + 2 * HEAD_TXT
    qkv_size = model_width * inner_width
    w_qkv = flat_slot[:qkv_size].reshape(model_width, inner_width)
    w_out = flat_slot[qkv_size : qkv_size + half_width * model_width].reshape(
        half_width, model_width
    )
    float_tokens = texts.astype(jnp.float32)
    normed = (
        float_tokens
        * lax.rsqrt(jnp.mean(float_tokens * float_tokens, axis=-1, keepdims=True) + norm_eps)
    ).astype(jnp.bfloat16)
    projections = jnp.einsum("btd,de->bte", normed, w_qkv, preferred_element_type=jnp.float32)
    positions = jnp.arange(token_count).astype(jnp.float32)
    queries = rotate_pairs(
        projections[..., :half_width].reshape(item_count, token_count, head_count, HEAD_TXT),
        positions,
    ).astype(jnp.bfloat16)
    key_rows = rotate_pairs(
        projections[..., half_width : half_width + HEAD_TXT].reshape(
            item_count, token_count, 1, HEAD_TXT
        ),
        positions,
    )[:, :, 0, :].astype(jnp.bfloat16)
    value_rows = projections[..., half_width + HEAD_TXT :].astype(jnp.bfloat16)
    scores = jnp.einsum(
        "bqhc,bkc->bhqk", queries, key_rows, preferred_element_type=jnp.float32
    ) / math.sqrt(HEAD_TXT)
    causal = jnp.arange(token_count)[:, None] >= jnp.arange(token_count)[None, :]
    scores = jnp.where(causal, scores, -1e30)
    probabilities = softmax_rows(scores)
    attended = jnp.einsum(
        "bhqk,bkc->bqhc", probabilities, value_rows, preferred_element_type=jnp.float32
    ).astype(jnp.bfloat16)
    attended = attended.reshape(item_count, token_count, half_width)
    projected = jnp.einsum("btc,cd->btd", attended, w_out, preferred_element_type=jnp.float32)
    return jnp.mean(projected, axis=1)


def merge_forward(embedded, stacked):
    first_rows = embedded.shape[1]
    float_embed = embedded.astype(jnp.float32)
    normed = (
        float_embed
        * lax.rsqrt(jnp.mean(float_embed * float_embed, axis=1, keepdims=True) + norm_eps)
    ).astype(jnp.bfloat16)
    hidden = jnp.dot(normed, stacked[:first_rows], preferred_element_type=jnp.float32)
    activated = gelu_value(hidden).astype(jnp.bfloat16)
    merged = jnp.dot(activated, stacked[first_rows:], preferred_element_type=jnp.float32).astype(
        jnp.bfloat16
    )
    return (normed, hidden, activated, merged)


def merge_backward(hidden, stacked, out_grad, first_rows):
    w_second = stacked[first_rows:]
    act_grad = lax.dot_general(
        out_grad, w_second, (((1,), (1,)), ((), ())), preferred_element_type=jnp.float32
    )
    return (act_grad * gelu_slope(hidden)).astype(jnp.bfloat16)


def item_loss(merged_row, book_rows, negatives):
    emb_width = merged_row.shape[0]
    quant_tau = math.sqrt(emb_width) / 2.0
    residual = merged_row * lax.rsqrt(jnp.mean(merged_row * merged_row) + norm_eps)
    quantized = jnp.zeros_like(merged_row)
    for level_index in range(book_rows.shape[0]):
        code_rows = book_rows[level_index]
        cross_terms = jnp.dot(code_rows, residual, precision=highest)
        logits = (2.0 * cross_terms - jnp.sum(code_rows * code_rows, axis=1)) / quant_tau
        logits = logits - lax.stop_gradient(jnp.max(logits))
        exp_logits = jnp.exp(logits)
        chosen = jnp.dot(exp_logits / jnp.sum(exp_logits), code_rows, precision=highest)
        residual = residual - chosen
        quantized = quantized + chosen
    recon_error = jnp.mean(residual * residual)
    anchor = quantized * lax.rsqrt(jnp.mean(quantized * quantized) + norm_eps)
    candidates = jnp.concatenate([merged_row[None, :], negatives.astype(jnp.float32)], axis=0)
    cand_unit = candidates * lax.rsqrt(
        jnp.mean(candidates * candidates, axis=1, keepdims=True) + norm_eps
    )
    similarity = jnp.dot(cand_unit, anchor, precision=highest) / (emb_width * contrast_temp)
    top_score = lax.stop_gradient(jnp.max(similarity))
    contrast = top_score + jnp.log(jnp.sum(jnp.exp(similarity - top_score))) - similarity[0]
    return contrast + beta_weight * recon_error


def stacked_term(columns, first_grad, second_grad, in_first):
    contract = (((0,), (0,)), ((), ()))
    first_term = lax.dot_general(columns, first_grad, contract, preferred_element_type=jnp.float32)
    second_term = lax.dot_general(
        columns, second_grad, contract, preferred_element_type=jnp.float32
    )
    return jnp.where(in_first[:, None], first_term, second_term)


def per_device(
    images,
    texts,
    section_weights,
    uniting_weights,
    codebooks,
    neg_bank,
    item_cats,
    cat_slot,
    neg_index,
):
    segment_index = lax.axis_index("segment")
    segment_count = lax.axis_size("segment")
    dp_index = lax.axis_index("dp")
    dp_count = lax.axis_size("dp")
    group_index = segment_index % 2
    item_count = images.shape[0]
    flat_slot = section_weights.reshape(-1)
    residual_flag = jnp.where(group_index == 0, 1.0, 0.0).astype(jnp.float32)

    def image_branch(operands):
        image_rows, text_rows, slot_rows = operands
        pooled = image_attention(image_rows, slot_rows) + residual_flag * jnp.mean(
            image_rows.astype(jnp.float32), axis=1
        )
        return jnp.concatenate(
            [pooled, jnp.zeros((item_count, text_rows.shape[2]), jnp.float32)], axis=1
        )

    def text_branch(operands):
        image_rows, text_rows, slot_rows = operands
        pooled = text_attention(text_rows, slot_rows) + residual_flag * jnp.mean(
            text_rows.astype(jnp.float32), axis=1
        )
        return jnp.concatenate(
            [jnp.zeros((item_count, image_rows.shape[2]), jnp.float32), pooled], axis=1
        )

    packed = lax.cond(segment_index < 2, image_branch, text_branch, (images, texts, flat_slot))
    embedded = lax.psum_scatter(packed, "segment", scatter_dimension=0, tiled=True).astype(
        jnp.bfloat16
    )
    stacked = lax.all_gather(uniting_weights, "dp", axis=0, tiled=True)
    first_rows = embedded.shape[1]
    cat_per_dev = codebooks.shape[0]
    slot_count = cat_per_dev * CAP
    row_total = item_cats.shape[1]
    cats_all = item_cats.reshape(-1)
    entry_count = cats_all.shape[0]
    entry_ids = jnp.arange(entry_count)
    category_match = cats_all[:, None] == jnp.arange(cat_slot.shape[0])[None, :]
    entry_slots = jnp.sum(jnp.where(category_match, cat_slot[None, :], 0), axis=1)
    entry_owner = entry_slots // cat_per_dev
    entry_local = entry_slots % cat_per_dev
    entry_row = entry_ids // row_total
    earlier = entry_ids[None, :] < entry_ids[:, None]
    same_cat = (cats_all[:, None] == cats_all[None, :]) & (entry_row[:, None] == entry_row[None, :])
    entry_rank = jnp.sum(jnp.where(earlier & same_cat, 1, 0), axis=1)
    entry_place = entry_local * CAP + entry_rank
    entry_position = entry_row * slot_count + entry_place
    owned = entry_owner == dp_index
    all_slots = segment_count * slot_count
    slot_match_all = owned[None, :] & (entry_position[None, :] == jnp.arange(all_slots)[:, None])
    view_match = lax.dynamic_slice(
        slot_match_all,
        (segment_index * slot_count, segment_index * row_total),
        (slot_count, row_total),
    )
    view_base = segment_index * row_total
    view_slots = view_match.shape[0]
    selection = view_match.astype(jnp.bfloat16)
    valid = jnp.sum(view_match.astype(jnp.float32), axis=1)
    slot_item = jnp.sum(
        jnp.where(view_match, jnp.arange(view_match.shape[1])[None, :] + view_base, 0), axis=1
    )
    slot_negs = jnp.take(neg_index.reshape(entry_count, -1), slot_item, axis=0)
    slot_local = jnp.arange(view_slots) % slot_count // CAP
    bank_rows = neg_bank.reshape(-1, neg_bank.shape[2])
    negatives = jnp.take(bank_rows, slot_local[:, None] * neg_bank.shape[1] + slot_negs, axis=0)
    loss_scale = 1.0 / math.sqrt(dp_count * item_count)

    def owner_objective(merged_float, books):
        per_row = jax.vmap(item_loss)(merged_float, books[slot_local], negatives)
        return jnp.sum(per_row * valid) * loss_scale

    gathered = jnp.dot(
        selection,
        lax.all_gather(embedded, "dp", axis=0, tiled=True),
        preferred_element_type=jnp.float32,
    )
    gathered = gathered.astype(jnp.bfloat16)
    normed_all, hidden_all, activated_all, merged_all = merge_forward(gathered, stacked)
    loss_local, pullback = jax.vjp(owner_objective, merged_all.astype(jnp.float32), codebooks)
    grad_all, book_grad = pullback(jnp.ones((), jnp.float32))
    out_grad = grad_all.astype(jnp.bfloat16)
    hidden_grad = merge_backward(hidden_all, stacked, out_grad, first_rows)
    joined = jnp.concatenate([normed_all, activated_all], axis=1)
    book_total, loss_owner = lax.psum((book_grad, loss_local), "segment")
    shard_rows = uniting_weights.shape[0]
    shard_start = dp_index * shard_rows
    shard_first = shard_start + jnp.arange(shard_rows) < first_rows
    joined_piece = lax.all_gather(joined, "dp", axis=0, tiled=True)
    first_piece = lax.all_gather(hidden_grad, "dp", axis=0, tiled=True)
    second_piece = lax.all_gather(out_grad, "dp", axis=0, tiled=True)
    columns = lax.dynamic_slice_in_dim(joined_piece, shard_start, shard_rows, 1)
    segment_grad = stacked_term(columns, first_piece, second_piece, shard_first)
    uniting_grad = lax.psum(segment_grad, "segment")
    return (uniting_grad, book_total, loss_owner.reshape(1))


def solution(mesh):
    placed = (
        P("dp", None, None),
        P("dp", None, None),
        P("segment", None, None),
        P("dp", None),
        P("dp", None, None, None),
        P("dp", None, None),
        P(),
        P(),
        P(),
    )
    return jax.shard_map(
        per_device,
        mesh=mesh,
        in_specs=placed,
        out_specs=(P("dp", None), P("dp", None, None, None), P("dp")),
        check_vma=False,
    )
```

profile of v0, /device:TPU:1, one launch (start us, length us, event | category | flops | bytes accessed | tf_op | source)
XLA Modules:
  0.0 945.5 jit_solution(2078119373908854478)
XLA Ops:
  9.9 64.5 %conditional.1 = (f32[8,2560]{1,0:T(8,128)S(1)}) conditional(s32[]{:T(128)} %convert_element_type.98, (bf16[8,64,1536]{2,1,0:T(8,128)(2,1)}, bf16[2752512]{0:T(1024)(128)(2,1)}, f32[]{:T(128)}) %tuple.55, (bf16[8,256,1024]{2,1,0:T(8,128)(2,1)}, bf16[2752512]{0:T(1024)(128)(2,1)}, f32[]{:T(128)}) %tuple.56), branch_computations={%region_2.8_spmd, %region_8.15_spmd} | conditional | flops 9714018304 | bytes 131555384 | solution.py:220
  10.4 3.0 convert_reduce_fusion.2
  13.4 3.5 fusion.43
  16.9 1.8 slice.87
  18.7 6.8 reshape.489
  25.5 9.9 %convolution_convert_fusion.1 = bf16[8,256,1536]{2,1,0:T(8,128)(2,1)S(1)} fusion(bf16[1024,1536,1]{1,0,2:T(8,128)(2,1)} %reshape.489, bf16[8,256,1024]{2,1,0:T(8,128)(2,1)} %get-tuple-element.27, f32[8,256]{1,0:T(8,128)S(1)} %add_rsqrt_fusion.1, f32[8,256]{1,0:T(8,128)S(1)} %broadcast_multiply_fusion), kind=kOutput, calls=%fused_computation.65 | convolution fusion | flops 6453985280 | bytes 13647872 | tf_op jit(solution)/shard_map/cond/branch_1_fun/bpd,de->bpe/dot_general | solution.py:60
  35.4 2.8 fusion.168
  38.2 4.0 copy.70
  42.2 3.9 copy.71
  46.1 10.6 %fusion.169 = (f32[8,8,256]{2,1,0:T(8,128)S(1)}, f32[8,8,256,256]{2,3,1,0:T(8,128)}) fusion(bf16[8,256,8,64]{1,3,2,0:T(8,128)(2,1)} %bitcast.232, bf16[8,256,8,64]{1,3,2,0:T(8,128)(2,1)} %bitcast.233), kind=kOutput, calls=%fused_computation.284 | convolution fusion | flops 549454080 | bytes 21037056 | tf_op jit(solution)/shard_map/cond/branch_1_fun/sub | solution.py:42
  56.7 2.4 copy.69
  59.1 9.4 fusion.52
  70.2 4.0 convolution_reduce_fusion.1
  74.5 13.8 %all-reduce.5 = bf16[8,2560]{1,0:T(8,128)(2,1)S(1)} all-reduce(f32[8,2560]{1,0:T(8,128)S(1)} %get-tuple-element.92), channel_id=2, replica_groups=mesh['segment'=4,'dp'=64] {'segment'}, use_global_device_ids=true, to_apply=%region_15.16.clone | all-reduce | flops 20480 | bytes 122880
  88.3 160.0 %all-gather = bf16[64,2,2560]{2,1,0:T(2,128)(2,1)S(1)} all-gather(bf16[1,2,2560]{2,1,0:T(2,128)(2,1)S(1)} %fusion.106), channel_id=1, replica_groups=mesh['segment'=4,'dp'=64] {'dp'}, dimensions={0}, use_global_device_ids=true | all-gather | bytes 665600 | tf_op jit(solution)/shard_map/all_gather | solution.py:269
  251.4 2.0 gather_fusion.1
  256.9 3.3 multiply_convert_fusion.1
  260.2 2.1 multiply_reduce_fusion.9
  271.8 1.8 broadcast_multiply_fusion.2
  278.0 2.2 fusion.80
  280.5 1.9 fusion.87
  288.7 1.8 multiply_reduce_fusion.1
  293.3 2.2 fusion.77
  295.5 148.0 %all-gather.2 = bf16[64,2,1024]{2,1,0:T(2,128)(2,1)S(1)} all-gather(bf16[1,2,1024]{2,1,0:T(2,128)(2,1)S(1)} %fusion.77), channel_id=1, replica_groups=mesh['segment'=4,'dp'=64] {'dp'}, dimensions={0}, use_global_device_ids=true | all-gather | bytes 266240 | tf_op jit(solution)/shard_map/all_gather | solution.py:284
  444.4 155.0 %all-gather.1 = bf16[64,2,3584]{2,1,0:T(2,128)(2,1)S(1)} all-gather(bf16[1,2,3584]{2,1,0:T(2,128)(2,1)} %maximum_bitcast_fusion), channel_id=1, replica_groups=mesh['segment'=4,'dp'=64] {'dp'}, dimensions={0}, use_global_device_ids=true | all-gather | bytes 931840 | tf_op jit(solution)/shard_map/all_gather | solution.py:283
  600.7 148.5 %all-gather.3 = bf16[64,2,1024]{2,1,0:T(2,128)(2,1)S(1)} all-gather(bf16[1,2,1024]{2,1,0:T(2,128)(2,1)} %bitcast.244), channel_id=1, replica_groups=mesh['segment'=4,'dp'=64] {'dp'}, dimensions={0}, use_global_device_ids=true | all-gather | bytes 266240 | tf_op jit(solution)/shard_map/all_gather | solution.py:285
  751.2 2.2 pad_add_fusion
  754.0 4.5 scatter_fusion
  759.8 1.8 convolution_select_fusion
  763.6 116.9 %psum.23 = f32[1]{0:T(128)} all-reduce(f32[1]{0:T(128)} %bitcast.57), channel_id=1, replica_groups=mesh['segment'=4,'dp'=64] {'segment'}, use_global_device_ids=true, to_apply=%region_40.41 | all-reduce | flops 1 | bytes 8 | tf_op jit(solution)/shard_map/psum | solution.py:279
  880.5 53.2 %all-reduce.9.cloned.1.call-done = (f32[56,1024]{1,0:T(8,128)}, f32[1,2,256,1024]{3,2,1,0:T(8,128)}) async-done(((f32[56,1024]{1,0:T(8,128)}, f32[1,2,256,1024]{3,2,1,0:T(8,128)}), (f32[56,1024]{1,0:T(8,128)}, f32[1,2,256,1024]{3,2,1,0:T(8,128)})) %all-reduce.9.cloned.1.call-update) | async-done | bytes 2326544 | tf_op jit(solution)/shard_map/psum | solution.py:288
  935.3 3.2 copy.190
  (167 shorter events, 42.3 us)
Async XLA Ops:
  7.2 244.2 %copy-start = (bf16[1,256,1024]{2,1,0:T(8,128)(2,1)S(1)}, bf16[1,256,1024]{2,1,0:T(8,128)(2,1)}, u32[]{:S(2)}) copy-start(bf16[1,256,1024]{2,1,0:T(8,128)(2,1)} %param.16) | copy-start | bytes 1572868
  7.2 249.7 %all-gather.6.cloned.1.call-start = ((), (), s32[]{:S(2)}) async-start(), calls=%async_computation | async-start | bytes 7454720 | tf_op jit(solution)/shard_map/all_gather | solution.py:224
  7.9 925.8 %all-reduce.9.cloned.1.call-start = ((), (), s32[]{:S(2)}) async-start(), calls=%async_computation.1 | async-start | bytes 4653056 | tf_op jit(solution)/shard_map/psum | solution.py:288
  10.4 6.5 copy-start.4
  74.4 174.1 %copy-start.15 = (s32[4,128,1]{1,2,0:T(1,128)S(1)}, s32[4,128,1]{1,2,0:T(1,128)}, u32[]{:S(2)}) copy-start(s32[4,128,1]{1,2,0:T(1,128)} %param.17) | copy-start | bytes 6148
  74.5 174.1 %copy-start.28 = (s32[64]{0:T(128)S(1)}, s32[64]{0:T(128)}, u32[]{:S(2)}) copy-start(s32[64]{0:T(128)} %param.18) | copy-start | bytes 772
  249.4 27.3 %copy-start.24 = (f32[2]{0:T(128)}, f32[2]{0:T(128)S(1)}, u32[]{:S(2)}) copy-start(f32[2]{0:T(128)S(1)} %get-tuple-element.44) | copy-start | bytes 28
  251.3 3.1 copy-start.6
  253.3 1.7 copy-start.8
  254.4 2.2 copy-start.7
  262.3 8.6 copy-start.2
  271.8 8.5 copy-start.11
  273.6 1.0 copy-start.5
  276.6 10.7 %copy-start.17 = (f32[2]{0:T(128)}, f32[2]{0:T(128)S(1)}, u32[]{:S(2)}) copy-start(f32[2]{0:T(128)S(1)} %get-tuple-element.72) | copy-start | bytes 28
  276.6 0.6 copy-start.22
  278.0 10.7 %copy-start.3 = (f32[2,128,1024]{2,0,1:T(2,128)S(1)}, f32[2,128,1024]{2,0,1:T(2,128)}, u32[]{:S(2)}) copy-start(f32[2,128,1024]{2,0,1:T(2,128)} %fusion.101) | copy-start | bytes 3145732
  285.6 6.2 copy-start.12
  285.6 6.3 slice-start
  292.7 0.6 copy-start.16
  600.7 149.9 %copy-start.13 = (f32[2,1024]{1,0:T(2,128)S(1)}, f32[2,1024]{1,0:T(2,128)}, u32[]{:S(2)}) copy-start(f32[2,1024]{1,0:T(2,128)} %copy-done.12) | copy-start | bytes 24580
  600.7 149.9 %copy-start.14 = (f32[2,1024]{1,0:T(2,128)S(1)}, f32[2,1024]{1,0:T(2,128)}, u32[]{:S(2)}) copy-start(f32[2,1024]{1,0:T(2,128)} %broadcast_multiply_fusion.4) | copy-start | bytes 24580
  600.7 149.9 %copy-start.19 = (f32[2,256]{1,0:T(2,128)S(1)}, f32[2,256]{1,0:T(2,128)}, u32[]{:S(2)}) copy-start(f32[2,256]{1,0:T(2,128)} %get-tuple-element.76) | copy-start | bytes 6148
  600.7 149.9 %copy-start.20 = (f32[2,256]{1,0:T(2,128)S(1)}, f32[2,256]{1,0:T(2,128)}, u32[]{:S(2)}) copy-start(f32[2,256]{1,0:T(2,128)} %broadcast_divide_fusion.1) | copy-start | bytes 6148
  600.7 149.9 %copy-start.21 = (f32[2,256]{1,0:T(2,128)S(1)}, f32[2,256]{1,0:T(2,128)}, u32[]{:S(2)}) copy-start(f32[2,256]{1,0:T(2,128)} %get-tuple-element.38) | copy-start | bytes 6148
  753.4 0.6 copy-start.27
  754.0 4.5 copy-start.10
  754.0 5.8 copy-start.29
  758.5 3.1 copy-start.1
  758.5 3.2 copy-start.18
  758.5 3.2 copy-start.23
  758.5 3.2 copy-start.25
  758.5 3.2 copy-start.26
Sparse Core Ops, SparseCore 0:
  11.5 144.8 all-gather.5
  761.8 171.8 all-reduce.8
where the time goes:
time: 953 us; the launch traced here: 946 us
  blocking collectives  742 us (78%)
  matrix products  59.7 us (6%)
  waiting for transfers between devices  53.9 us (6%)
  local copies, waits for them, and re-layouts  39.2 us (4%)
  other arithmetic  33.6 us (4%)
  between operations  16.1 us (2%)
    all_gather x1, blocking collectives, per_device(): lax.all_gather(embedded, 'dp', axis=0, tiled=True)  160 us
    all_gather x1, blocking collectives, per_device(): joined_piece = lax.all_gather(joined, 'dp', axis=0, tiled=True)  155 us
    all_gather x1, blocking collectives, per_device(): second_piece = lax.all_gather(out_grad, 'dp', axis=0, tiled=True)  149 us
    all_gather x1, blocking collectives, per_device(): first_piece = lax.all_gather(hidden_grad, 'dp', axis=0, tiled=True)  148 us
    psum x1, blocking collectives, per_device(): book_total, loss_owner = lax.psum((book_grad, loss_local), 'segment')  117 us
    psum x1, waiting for transfers between devices, per_device(): uniting_grad = lax.psum(segment_grad, 'segment')  53.2 us
  transfers between devices with their start and end apart: 2, of which 1 were waited for; matrix products, arithmetic and copies ran while one was open for 8% of the time, Pallas kernels for 0%

commit v1 on v0

--- a/solution.py
+++ b/solution.py
@@ -3,6 +3,8 @@
 import jax
 import jax.numpy as jnp
 from jax import lax
+from jax.experimental import pallas as pl
+from jax.experimental.pallas import tpu as pltpu
 from jax.sharding import PartitionSpec as P
 
 HEAD_IMG = 64
@@ -179,6 +181,66 @@
     return jnp.where(in_first[:, None], first_term, second_term)
 
 
+def gather_body(count, block_ref, out_ref, local_sem, send_sems, recv_sems):
+    me = lax.axis_index("dp")
+    barrier = pltpu.get_barrier_semaphore()
+
+    def greet(step, carry):
+        peer = lax.rem(me + step, count)
+        pl.semaphore_signal(
+            barrier, inc=1, device_id={"dp": peer}, device_id_type=pl.DeviceIdType.MESH
+        )
+        return carry
+
+    lax.fori_loop(1, count, greet, 0)
+    own = pltpu.make_async_copy(block_ref, out_ref.at[me], local_sem)
+    own.start()
+    pl.semaphore_wait(barrier, count - 1)
+
+    def copy_to(step):
+        peer = lax.rem(me + step, count)
+        return pltpu.make_async_remote_copy(
+            src_ref=block_ref,
+            dst_ref=out_ref.at[me],
+            send_sem=send_sems.at[step],
+            recv_sem=recv_sems.at[step],
+            device_id={"dp": peer},
+            device_id_type=pl.DeviceIdType.MESH,
+        )
+
+    def send(step, carry):
+        copy_to(step).start()
+        return carry
+
+    def finish(step, carry):
+        copy_to(step).wait()
+        return carry
+
+    lax.fori_loop(1, count, send, 0)
+    lax.fori_loop(1, count, finish, 0)
+    own.wait()
+
+
+def gather_dp(block, collective_id):
+    count = lax.axis_size("dp")
+    gathered = pl.pallas_call(
+        lambda *refs: gather_body(count, *refs),
+        out_shape=jax.ShapeDtypeStruct((count,) + block.shape, block.dtype),
+        in_specs=[pl.BlockSpec(memory_space=pltpu.VMEM)],
+        out_specs=pl.BlockSpec(memory_space=pltpu.VMEM),
+        scratch_shapes=[
+            pltpu.SemaphoreType.DMA,
+            pltpu.SemaphoreType.DMA((count,)),
+            pltpu.SemaphoreType.DMA((count,)),
+        ],
+        compiler_params=pltpu.CompilerParams(
+            collective_id=collective_id, has_side_effects=True, vmem_limit_bytes=40 << 20
+        ),
+        name=f"gather_{collective_id}",
+    )(block)
+    return gathered.reshape((-1,) + block.shape[1:])
+
+
 def per_device(
     images,
     texts,
@@ -221,7 +283,7 @@
     embedded = lax.psum_scatter(packed, "segment", scatter_dimension=0, tiled=True).astype(
         jnp.bfloat16
     )
-    stacked = lax.all_gather(uniting_weights, "dp", axis=0, tiled=True)
+    stacked = gather_dp(uniting_weights, 1)
     first_rows = embedded.shape[1]
     cat_per_dev = codebooks.shape[0]
     slot_count = cat_per_dev * CAP
@@ -266,7 +328,7 @@
 
     gathered = jnp.dot(
         selection,
-        lax.all_gather(embedded, "dp", axis=0, tiled=True),
+        gather_dp(embedded, 2),
         preferred_element_type=jnp.float32,
     )
     gathered = gathered.astype(jnp.bfloat16)
@@ -280,9 +342,9 @@
     shard_rows = uniting_weights.shape[0]
     shard_start = dp_index * shard_rows
     shard_first = shard_start + jnp.arange(shard_rows) < first_rows
-    joined_piece = lax.all_gather(joined, "dp", axis=0, tiled=True)
-    first_piece = lax.all_gather(hidden_grad, "dp", axis=0, tiled=True)
-    second_piece = lax.all_gather(out_grad, "dp", axis=0, tiled=True)
+    joined_piece = gather_dp(joined, 3)
+    first_piece = gather_dp(hidden_grad, 4)
+    second_piece = gather_dp(out_grad, 5)
     columns = lax.dynamic_slice_in_dim(joined_piece, shard_start, shard_rows, 1)
     segment_grad = stacked_term(columns, first_piece, second_piece, shard_first)
     uniting_grad = lax.psum(segment_grad, "segment")

time: 953 us -> 542 us (0.57)
  blocking collectives: 742 us -> 27.5 us
  Pallas kernels: 0 us -> 299 us
    all_gather x4 -> x0, blocking collectives: 612 us -> none  [the longest x1 160 us: per_device(): lax.all_gather(embedded, 'dp', axis=0, tiled=True)]
    pallas_call x0 -> x5, Pallas kernels: none -> 299 us  [gather_dp(): pl.pallas_call(lambda *refs: gather_body(count, *refs), out_shape=jax.Sha...]
    psum x1, blocking collectives: 117 us -> 14.2 us  [per_device(): book_total, loss_owner = lax.psum((book_grad, loss_local), 'segment')]
  transfers between devices with their start and end apart: 2 -> 1, of which waited for: 1 -> 1; matrix products, arithmetic and copies ran while one was open for 8% -> 0% of each run, Pallas kernels for 0% -> 0%
where the time goes in v1:
time: 542 us; the launch traced here: 536 us
  Pallas kernels  299 us (55%)
  matrix products  56.9 us (10%)
  waiting for transfers between devices  56 us (10%)
  local copies, waits for them, and re-layouts  48 us (9%)
  other arithmetic  31.4 us (6%)
  blocking collectives  27.5 us (5%)
  between operations  16.2 us (3%)
    pallas_call x5, Pallas kernels, gather_dp(): pl.pallas_call(lambda *refs: gather_body(count, *refs), out_shape=jax.Sha...  299 us
    psum x1, waiting for transfers between devices, per_device(): uniting_grad = lax.psum(segment_grad, 'segment')  56 us
    psum x1, blocking collectives, per_device(): book_total, loss_owner = lax.psum((book_grad, loss_local), 'segment')  14.2 us
    unnamed x1, blocking collectives  13.4 us
    unnamed x68, local copies, waits for them, and re-layouts  11.2 us
  transfers between devices with their start and end apart: 1, of which 1 were waited for; matrix products, arithmetic and copies ran while one was open for 0% of the time, Pallas kernels for 0%

profile of v1, /device:TPU:1, one launch (start us, length us, event | category | flops | bytes accessed | tf_op | source)
XLA Modules:
  0.0 536.2 jit_solution(12127194669133141323)
XLA Ops:
  7.3 1.9 slice_bitcast_fusion.3
  12.8 69.2 %conditional.1 = (f32[8,2560]{1,0:T(8,128)S(1)}) conditional(s32[]{:T(128)} %convert_element_type.98, (bf16[8,64,1536]{2,1,0:T(8,128)(2,1)}, bf16[2752512]{0:T(1024)(128)(2,1)}, f32[]{:T(128)}) %tuple.54, (bf16[8,256,1024]{2,1,0:T(8,128)(2,1)}, bf16[2752512]{0:T(1024)(128)(2,1)}, f32[]{:T(128)}) %tuple.55), branch_computations={%region_2.8_spmd, %region_8.15_spmd} | conditional | flops 9714018304 | bytes 131555384 | solution.py:282
  13.3 3.0 convert_reduce_fusion.2
  16.3 3.5 fusion.43
  19.8 1.8 slice.87
  21.6 6.8 %reshape.501 = bf16[1024,1536,1]{1,0,2:T(8,128)(2,1)} reshape(bf16[1572864]{0:T(1024)(128)(2,1)} %slice.87) | data formatting | bytes 6291456 | tf_op jit(solution)/shard_map/cond/branch_1_fun/slice | solution.py:54
  28.4 9.9 %convolution_convert_fusion.1 = bf16[8,256,1536]{2,1,0:T(8,128)(2,1)S(1)} fusion(bf16[1024,1536,1]{1,0,2:T(8,128)(2,1)} %reshape.501, bf16[8,256,1024]{2,1,0:T(8,128)(2,1)} %get-tuple-element.27, f32[8,256]{1,0:T(8,128)S(1)} %add_rsqrt_fusion.1, f32[8,256]{1,0:T(8,128)S(1)} %broadcast_multiply_fusion), kind=kOutput, calls=%fused_computation.65 | convolution fusion | flops 6453985280 | bytes 13647872 | tf_op jit(solution)/shard_map/cond/branch_1_fun/bpd,de->bpe/dot_general | solution.py:62
  38.3 3.0 fusion.164
  41.3 3.9 copy.70
  45.2 3.9 copy.71
  49.1 10.6 %fusion.165 = (f32[8,8,256]{2,1,0:T(8,128)S(1)}, f32[8,8,256,256]{2,3,1,0:T(8,128)}) fusion(bf16[8,256,8,64]{1,3,2,0:T(8,128)(2,1)} %bitcast.229, bf16[8,256,8,64]{1,3,2,0:T(8,128)(2,1)} %bitcast.230), kind=kOutput, calls=%fused_computation.282 | convolution fusion | flops 549454080 | bytes 21037056 | tf_op jit(solution)/shard_map/cond/branch_1_fun/sub | solution.py:44
  59.7 3.9 copy.69
  63.6 9.4 %fusion.52 = bf16[8,8,64,256]{3,2,1,0:T(8,128)(2,1)} fusion(bf16[8,256,8,64]{1,3,2,0:T(8,128)(2,1)} %bitcast.231, f32[8,8,256,256]{2,3,1,0:T(8,128)} %get-tuple-element.66, f32[8,8,256]{2,1,0:T(8,128)S(1)} %get-tuple-element.65), kind=kOutput, calls=%fused_computation.70 | convolution fusion | flops 546308096 | bytes 21037056 | tf_op jit(solution)/shard_map/cond/branch_1_fun/bhqk,bkhc->bqhc/dot_general | solution.py:76
  73.0 2.3 slice.92
  75.2 2.3 reshape.502
  77.5 4.2 convolution_reduce_fusion.1
  82.0 13.4 %all-reduce.5 = bf16[8,2560]{1,0:T(8,128)(2,1)S(1)} all-reduce(f32[8,2560]{1,0:T(8,128)S(1)} %get-tuple-element.94), channel_id=2, replica_groups=mesh['segment'=4,'dp'=64] {'segment'}, use_global_device_ids=true, to_apply=%region_15.16.clone | all-reduce | flops 20480 | bytes 122880
  96.7 26.9 %gather_2.1 = bf16[64,2,2560]{2,1,0:T(2,128)(2,1)S(1)} custom-call(bf16[2,2560]{1,0:T(2,128)(2,1)S(1)} %dynamic-slice_convert_fusion.refs_0_), custom_call_target="tpu_custom_call" | custom-call | tf_op jit(solution)/shard_map/gather_2/pallas_call | solution.py:226
  126.0 179.9 %gather_1.1 = bf16[64,56,1024]{2,1,0:T(8,128)(2,1)S(1)} custom-call(bf16[56,1024]{1,0:T(8,128)(2,1)S(1)} %copy-done.2), custom_call_target="tpu_custom_call" | custom-call | tf_op jit(solution)/shard_map/gather_1/pallas_call | solution.py:226
  306.8 2.1 copy-done.1
  328.5 2.2 fusion.77
  342.0 46.0 %gather_5.1 = bf16[64,2,1024]{2,1,0:T(2,128)(2,1)S(1)} custom-call(bf16[2,1024]{1,0:T(2,128)(2,1)S(1)} %fusion.112.refs_0_), custom_call_target="tpu_custom_call" | custom-call | tf_op jit(solution)/shard_map/gather_5/pallas_call | solution.py:226
  388.0 2.2 fusion.68.refs_0_
  390.3 18.0 %gather_4.1 = bf16[64,2,1024]{2,1,0:T(2,128)(2,1)S(1)} custom-call(bf16[2,1024]{1,0:T(2,128)(2,1)S(1)} %fusion.68.refs_0_), custom_call_target="tpu_custom_call" | custom-call | tf_op jit(solution)/shard_map/gather_4/pallas_call | solution.py:226
  409.1 28.7 %gather_3.1 = bf16[64,2,3584]{2,1,0:T(2,128)(2,1)S(1)} custom-call(bf16[2,3584]{1,0:T(2,128)(2,1)S(1)} %pad_maximum_fusion.3.refs_0_), custom_call_target="tpu_custom_call" | custom-call | tf_op jit(solution)/shard_map/gather_3/pallas_call | solution.py:226
  439.3 2.3 fusion.58
  441.6 2.2 pad_add_fusion
  444.5 4.5 scatter_fusion
  450.3 1.8 convolution_select_fusion
  454.2 14.2 %psum.23 = f32[1]{0:T(128)} all-reduce(f32[1]{0:T(128)} %bitcast.54), channel_id=1, replica_groups=mesh['segment'=4,'dp'=64] {'segment'}, use_global_device_ids=true, to_apply=%region_40.41 | all-reduce | flops 1 | bytes 8 | tf_op jit(solution)/shard_map/psum | solution.py:341
  468.3 56.0 %all-reduce.9.cloned.1.call-done = (f32[56,1024]{1,0:T(8,128)}, f32[1,2,256,1024]{3,2,1,0:T(8,128)}) async-done(((f32[56,1024]{1,0:T(8,128)}, f32[1,2,256,1024]{3,2,1,0:T(8,128)}), (f32[56,1024]{1,0:T(8,128)}, f32[1,2,256,1024]{3,2,1,0:T(8,128)})) %all-reduce.9.cloned.1.call-update) | async-done | bytes 2326544 | tf_op jit(solution)/shard_map/psum | solution.py:350
  526.0 3.2 copy.190
  (172 shorter events, 45.4 us)
Async XLA Ops:
  7.2 311.6 %copy-start = (bf16[1,256,1024]{2,1,0:T(8,128)(2,1)S(1)}, bf16[1,256,1024]{2,1,0:T(8,128)(2,1)}, u32[]{:S(2)}) copy-start(bf16[1,256,1024]{2,1,0:T(8,128)(2,1)} %param.16) | copy-start | bytes 1572868
  7.2 517.2 %all-reduce.9.cloned.1.call-start = ((), (), s32[]{:S(2)}) async-start(), calls=%async_computation | async-start | bytes 4653056 | tf_op jit(solution)/shard_map/psum | solution.py:350
  7.3 2.3 copy-start.10
  9.5 324.6 %copy-start.3 = (f32[256,1024]{1,0:T(8,128)}, f32[256,1024]{1,0:T(8,128)S(1)}, u32[]{:S(2)}) copy-start(f32[256,1024]{1,0:T(8,128)S(1)} %get-tuple-element.68) | copy-start | bytes 3145732
  9.5 0.7 copy-start.32
  11.0 316.3 %copy-start.28 = (f32[2]{0:T(128)}, f32[2]{0:T(128)S(1)}, u32[]{:S(2)}) copy-start(f32[2]{0:T(128)S(1)} %get-tuple-element.44) | copy-start | bytes 28
  12.8 82.6 %copy-start.34 = (u32[256]{0:T(256)S(1)}, u32[256]{0:T(256)}, u32[]{:S(2)}) copy-start(u32[256]{0:T(256)} %constant.245) | copy-start | bytes 3076
  13.3 6.5 %copy-start.8 = (bf16[2752512]{0:T(1024)(128)(2,1)S(1)}, bf16[2752512]{0:T(1024)(128)(2,1)}, u32[]{:S(2)}) copy-start(bf16[2752512]{0:T(1024)(128)(2,1)} %get-tuple-element.19) | copy-start | bytes 16515076 | tf_op jit(solution)/shard_map/cond
  82.0 44.0 %copy-start.2 = (bf16[56,1024]{1,0:T(8,128)(2,1)S(1)}, bf16[56,1024]{1,0:T(8,128)(2,1)}, u32[]{:S(2)}) copy-start(bf16[56,1024]{1,0:T(8,128)(2,1)} %refs_0_.1) | copy-start | bytes 344068
  305.9 3.0 copy-start.1
  313.4 22.0 %copy-start.14 = (f32[2,1024]{1,0:T(2,128)}, f32[2,1024]{1,0:T(2,128)S(1)}, u32[]{:S(2)}) copy-start(f32[2,1024]{1,0:T(2,128)S(1)} %bitcast_subtract_fusion.1) | copy-start | bytes 24580
  320.6 1.0 copy-start.6
  322.4 8.3 %copy-start.13 = (f32[2,129]{0,1:T(8,128)}, f32[2,129]{0,1:T(8,128)S(1)}, u32[]{:S(2)}) copy-start(f32[2,129]{0,1:T(8,128)S(1)} %copy.77) | copy-start | bytes 3100
  324.2 1.0 copy-start.9
  327.3 3.5 copy-start.26
  328.5 9.6 %copy-start.7 = (f32[2,128,1024]{2,0,1:T(2,128)S(1)}, f32[2,128,1024]{2,0,1:T(2,128)}, u32[]{:S(2)}) copy-start(f32[2,128,1024]{2,0,1:T(2,128)} %copy-done.6) | copy-start | bytes 3145732
  330.9 5.1 copy-start.16
  336.1 5.2 slice-start
  390.3 49.0 %copy-start.15 = (f32[2,1024]{1,0:T(2,128)S(1)}, f32[2,1024]{1,0:T(2,128)}, u32[]{:S(2)}) copy-start(f32[2,1024]{1,0:T(2,128)} %copy-done.14) | copy-start | bytes 24580
  390.3 49.0 %copy-start.17 = (f32[2,1024]{1,0:T(2,128)S(1)}, f32[2,1024]{1,0:T(2,128)}, u32[]{:S(2)}) copy-start(f32[2,1024]{1,0:T(2,128)} %copy-done.16) | copy-start | bytes 24580
  390.3 49.0 %copy-start.18 = (f32[2,1024]{1,0:T(2,128)S(1)}, f32[2,1024]{1,0:T(2,128)}, u32[]{:S(2)}) copy-start(f32[2,1024]{1,0:T(2,128)} %broadcast_multiply_fusion.4) | copy-start | bytes 24580
  390.3 49.0 %copy-start.22 = (f32[2,256]{1,0:T(2,128)S(1)}, f32[2,256]{1,0:T(2,128)}, u32[]{:S(2)}) copy-start(f32[2,256]{1,0:T(2,128)} %get-tuple-element.74) | copy-start | bytes 6148
  390.3 49.0 %copy-start.23 = (f32[2,256]{1,0:T(2,128)S(1)}, f32[2,256]{1,0:T(2,128)}, u32[]{:S(2)}) copy-start(f32[2,256]{1,0:T(2,128)} %broadcast_divide_fusion.1) | copy-start | bytes 6148
  390.3 49.0 %copy-start.24 = (f32[2,256]{1,0:T(2,128)S(1)}, f32[2,256]{1,0:T(2,128)}, u32[]{:S(2)}) copy-start(f32[2,256]{1,0:T(2,128)} %broadcast_divide_fusion) | copy-start | bytes 6148
  390.3 49.0 %copy-start.25 = (f32[2,256]{1,0:T(2,128)S(1)}, f32[2,256]{1,0:T(2,128)}, u32[]{:S(2)}) copy-start(f32[2,256]{1,0:T(2,128)} %get-tuple-element.36) | copy-start | bytes 6148
  444.5 4.5 copy-start.12
  444.5 5.8 %copy-start.33 = (pred[56]{0:T(512)(128)(4,1)S(1)}, pred[56]{0:T(512)(128)(4,1)}, u32[]{:S(2)}) copy-start(pred[56]{0:T(512)(128)(4,1)} %add_compare_fusion) | copy-start | bytes 172
  449.0 3.1 copy-start.5
  449.0 3.2 copy-start.21
  449.0 3.2 copy-start.27
  449.0 3.2 copy-start.29
  449.0 3.2 copy-start.30
  (3 other events, 1.9 us)
Sparse Core Ops, SparseCore 0:
  452.3 72.0 all-reduce.8

commit v2 on v0

v2 whole, which is shorter than its diff:
```python
import math

import jax
import jax.numpy as jnp
import numpy as np
from jax import lax
from jax.experimental import pallas as pl
from jax.experimental.pallas import tpu as pltpu
from jax.sharding import PartitionSpec as P

MESH = pl.DeviceIdType.MESH
BF = jnp.bfloat16
F32 = jnp.float32
HEAD_IMG = 64
HEAD_TXT = 128
CAP = 2
SEG = 4
NZ = 8
NQ = 8
NDP = 64

norm_eps = 1e-06
rope_theta = 1000000.0
contrast_temp = 0.1
NT = (((1,), (1,)), ((), ()))
TN = (((0,), (0,)), ((), ()))
NN = (((1,), (0,)), ((), ()))


def dot(a, b, dims=NN):
    return lax.dot_general(a, b, dims, preferred_element_type=F32)


def iota(shape, axis):
    return lax.broadcasted_iota(jnp.int32, shape, axis)


def split(a):
    high = a.astype(BF)
    return high, (a - high.astype(F32)).astype(BF)


def dot3(a, pair, dims):
    rows = a.shape[0]
    high, low = split(a)
    both = dot(jnp.concatenate([high, low], axis=0), pair[0], dims)
    return both[:rows] + both[rows:] + dot(high, pair[1], dims)


def unit_scale(a):
    return lax.rsqrt(jnp.mean(a * a, axis=1, keepdims=True) + norm_eps)


def relayout(slot, stage, first, rows, blocks, dest):
    group = 64

    def step(index, carry):
        base = pl.multiple_of(first + index * (group * blocks), 64)
        stage[pl.ds(0, group * blocks), :] = slot[pl.ds(base, group * blocks), :].astype(F32)
        at = pl.multiple_of(index * group, group)
        for block in range(blocks):
            dest[pl.ds(at, group), block * 128 : (block + 1) * 128] = stage[
                pl.ds(block, group, stride=blocks), :
            ].astype(BF)
        return carry

    lax.fori_loop(0, rows // group, step, 0)


def attend(scores):
    size = scores.shape[0]
    total = None
    for start in range(0, size, 64):
        part = scores[start : start + 64]
        top = jnp.max(part, axis=1, keepdims=True)
        probs = jnp.exp(part - top)
        probs = probs * (1.0 / jnp.sum(probs, axis=1, keepdims=True))
        folded = jnp.sum(probs.reshape(8, 8, size), axis=0)
        total = folded if total is None else total + folded
    return jnp.sum(total, axis=0, keepdims=True)


def image_part(flag, img, slot, stage, wi, wio, xn, qk, ysum, means, pool_row, img_sems, images):
    relayout(slot, stage, 0, 1024, 12, wi)
    relayout(slot, stage, 12288, 512, 8, wio)
    lane = iota((1, 128), 1)
    masks = (lane < 64, lane >= 64)

    def item(index, carry):
        pltpu.make_async_copy(images.at[index], img.at[index], img_sems.at[index]).wait()
        total = None
        for start in range(0, 256, 32):
            rows = img[index, start : start + 32, :].astype(F32)
            part = jnp.sum(rows.reshape(4, 8, 1024), axis=0)
            total = part if total is None else total + part
            centred = rows - jnp.mean(rows, axis=1, keepdims=True)
            xn[start : start + 32, 0:1024] = (centred * unit_scale(centred)).astype(BF)
        means[pl.ds(index, 1), 0:1024] = jnp.sum(total, axis=0, keepdims=True) * (1.0 / 256.0)
        normed = xn[:, 0:1024]
        qk[...] = dot(normed, wi[:, 0:1024]).astype(BF)
        sums = []
        for pair in range(4):
            query = qk[:, pair * 128 : (pair + 1) * 128] * BF(1.0 / math.sqrt(HEAD_IMG))
            keys = qk[:, 512 + pair * 128 : 512 + (pair + 1) * 128]
            for mask in masks:
                sums.append(attend(dot(jnp.where(mask, query, BF(0.0)), keys, NT)))
        weights = (jnp.concatenate(sums, axis=0) * (1.0 / 256.0)).astype(BF)
        ysum[pl.ds(pl.multiple_of(index * 8, 8), 8), :] = dot(weights, normed)
        return carry

    lax.fori_loop(0, 8, item, 0)
    values = dot(ysum[...].astype(BF), wi[:, 1024:1536])
    head = iota((64, 512), 0) % 8
    own = jnp.where(iota((64, 512), 1) // HEAD_IMG == head, values, 0.0)
    attended = jnp.sum(own.reshape(8, 8, 512), axis=1).astype(BF)
    pool_row[:, 0:1024] = dot(attended, wio[...]) + flag * means[:, 0:1024]
    pool_row[:, 1024:1536] = jnp.zeros((8, 512), F32)


def text_part(flag, txt, slot, stage, wt, wto, xn, cos_ref, sin_ref, attended, means, pool_row):
    relayout(slot, stage, 0, 1536, 8, wt)
    relayout(slot, stage, 12288, 768, 12, wto)
    attended[...] = jnp.zeros((8, 768), F32)
    means[...] = jnp.zeros((8, 1536), F32)
    row, column = iota((256, 256), 0), iota((256, 256), 1)
    causal = (row // 64 == column // 64) & (column <= row)
    cosine, sine = cos_ref[...], sin_ref[...]

    def rotate(tensor):
        return (tensor * cosine + pltpu.roll(tensor, 64, 1) * sine).astype(BF)

    def half(index, carry):
        base = pl.multiple_of(index * 256, 256)
        for start in range(0, 256, 32):
            rows = txt[pl.ds(base + start, 32), :].astype(F32)
            xn[start : start + 32, :] = (rows * unit_scale(rows)).astype(BF)
        member = jnp.where(
            iota((8, 256), 0) == index * 4 + iota((8, 256), 1) // 64, 1.0 / 64.0, 0.0
        )
        means[...] += dot(member.astype(BF), txt[pl.ds(base, 256), :])
        projected = dot(xn[...], wt[...])
        keys = rotate(projected[:, 768:896])
        values = projected[:, 896:1024].astype(BF)
        for head in range(6):
            query = rotate(projected[:, head * 128 : (head + 1) * 128])
            scores = dot(query, keys, NT) * (1.0 / math.sqrt(HEAD_TXT))
            weights = attend(jnp.where(causal, scores, -1e30))
            attended[:, head * 128 : (head + 1) * 128] += dot(
                (weights * member).astype(BF), values
            )
        return carry

    lax.fori_loop(0, 2, half, 0)
    pool_row[...] = dot(attended[...].astype(BF), wto[...]) + flag * means[...]


def encode_body(
    images, texts, section, unit, cos_ref, sin_ref,
    pool, wcol,
    slot, stage, wi, wio, wt, wto, img, txt, xn, qk, ysum, means, attended, mine,
    slot_sem, img_sems, txt_sem, own_sem, w_send, w_recv, s_send, s_recv,
):
    seg, me = lax.axis_index("segment"), lax.axis_index("dp")
    block = seg ^ (2 * (me % 2))
    is_image = seg < 2
    flag = jnp.where(seg % 2 == 0, 1.0, 0.0)
    barrier = pltpu.get_barrier_semaphore()

    def peer_of(step):
        peer = lax.rem(me + step, NDP)
        return {"segment": block ^ (2 * (peer % 2)), "dp": peer}

    def greet(step, carry):
        pl.semaphore_signal(barrier, inc=1, device_id=peer_of(step), device_id_type=MESH)
        return carry

    lax.fori_loop(1, NDP, greet, 0)
    for step in range(1, SEG):
        pl.semaphore_signal(
            barrier, inc=1, device_id={"segment": lax.rem(seg + step, SEG)}, device_id_type=MESH
        )
    slot_copy = pltpu.make_async_copy(section, slot, slot_sem)
    slot_copy.start()
    txt_copy = pltpu.make_async_copy(texts, txt, txt_sem)

    @pl.when(is_image)
    def _():
        def fetch(index, carry):
            pltpu.make_async_copy(images.at[index], img.at[index], img_sems.at[index]).start()
            return carry

        lax.fori_loop(0, 8, fetch, 0)

    @pl.when(jnp.logical_not(is_image))
    def _():
        txt_copy.start()

    columns = pl.ds(pl.multiple_of(block * 256, 256), 256)
    own = pltpu.make_async_copy(unit.at[:, columns], wcol.at[me], own_sem)
    own.start()
    pl.semaphore_wait(barrier, NDP - 1 + SEG - 1)

    def w_copy(step):
        return pltpu.make_async_remote_copy(
            src_ref=unit.at[:, columns],
            dst_ref=wcol.at[me],
            send_sem=w_send.at[step],
            recv_sem=w_recv.at[step],
            device_id=peer_of(step),
            device_id_type=MESH,
        )

    def w_start(step, carry):
        w_copy(step).start()
        return carry

    lax.fori_loop(1, NDP, w_start, 0)
    slot_copy.wait()

    @pl.when(is_image)
    def _():
        image_part(
            flag, img, slot, stage, wi, wio, xn, qk, ysum, means, mine, img_sems, images
        )

    @pl.when(jnp.logical_not(is_image))
    def _():
        txt_copy.wait()
        text_part(flag, txt, slot, stage, wt, wto, xn, cos_ref, sin_ref, attended, means, mine)

    def pool_copy(step):
        return pltpu.make_async_remote_copy(
            src_ref=mine,
            dst_ref=pool.at[seg],
            send_sem=s_send.at[step],
            recv_sem=s_recv.at[step],
            device_id={"segment": lax.rem(seg + step, SEG)},
            device_id_type=MESH,
        )

    for step in range(1, SEG):
        pool_copy(step).start()
    pool[seg] = mine[...]

    def w_finish(step, carry):
        w_copy(step).wait()
        return carry

    lax.fori_loop(1, NDP, w_finish, 0)
    own.wait()
    for step in range(1, SEG):
        pool_copy(step).wait()


def encode(images, texts, section, unit):
    half = HEAD_TXT // 2
    exponents = np.arange(half, dtype=np.float32) * np.float32(2.0 / HEAD_TXT)
    inverse = np.exp(np.float32(-math.log(rope_theta)) * exponents).astype(np.float32)
    angles = np.arange(64, dtype=np.float32)[:, None] * inverse[None, :]
    cosine = np.tile(np.cos(angles), (4, 2)).astype(np.float32)
    sine = np.tile(np.concatenate([-np.sin(angles), np.sin(angles)], axis=1), (4, 1))
    anywhere = pl.BlockSpec(memory_space=pl.ANY)
    vmem = pl.BlockSpec(memory_space=pltpu.VMEM)
    dma = pltpu.SemaphoreType.DMA
    return pl.pallas_call(
        encode_body,
        out_shape=(
            jax.ShapeDtypeStruct((SEG, 8, 1536), F32),
            jax.ShapeDtypeStruct((NDP, 56, 256), BF),
        ),
        in_specs=[anywhere, anywhere, anywhere, vmem, vmem, vmem],
        out_specs=(vmem, anywhere),
        scratch_shapes=[
            pltpu.VMEM((21504, 128), BF),
            pltpu.VMEM((768, 128), F32),
            pltpu.VMEM((1024, 1536), BF),
            pltpu.VMEM((512, 1024), BF),
            pltpu.VMEM((1536, 1024), BF),
            pltpu.VMEM((768, 1536), BF),
            pltpu.VMEM((8, 256, 1024), BF),
            pltpu.VMEM((512, 1536), BF),
            pltpu.VMEM((256, 1536), BF),
            pltpu.VMEM((256, 1024), BF),
            pltpu.VMEM((64, 1024), F32),
            pltpu.VMEM((8, 1536), F32),
            pltpu.VMEM((8, 768), F32),
            pltpu.VMEM((8, 1536), F32),
            dma, dma((8,)), dma, dma, dma((NDP,)), dma((NDP,)), dma((SEG,)), dma((SEG,)),
        ],
        compiler_params=pltpu.CompilerParams(
            collective_id=0, has_side_effects=True, vmem_limit_bytes=60 << 20
        ),
        name="encode",
    )(
        images,
        texts.reshape(512, 1536),
        section.reshape(21504, 128),
        unit,
        jnp.asarray(cosine, F32),
        jnp.asarray(sine, F32),
    )


def softmax(logits):
    exps = jnp.exp(logits - jnp.max(logits, axis=1, keepdims=True))
    return exps / jnp.sum(exps, axis=1, keepdims=True)


def row_total(a):
    return jnp.sum(a, axis=1, keepdims=True)


def slot_ids(cats, rows, keys, cats_col, slot_col):
    named = iota((NDP, 512), 0) == cats
    owner = jnp.sum(jnp.where(named, slot_col, 0.0), axis=0, keepdims=True)
    rank = jnp.zeros((8, 512), F32)
    for start in range(0, 512, 64):
        entry = iota((64, 1), 0) + start
        earlier = (
            (cats_col[start : start + 64] == cats)
            & (entry // 128 == rows)
            & (entry % 128 < keys)
        )
        rank = rank + jnp.sum(jnp.where(earlier, 1.0, 0.0).reshape(8, 8, 512), axis=0)
    rank = jnp.sum(rank, axis=0, keepdims=True)
    return owner.astype(jnp.int32), rows * CAP + rank.astype(jnp.int32)


def quantize(m, valid, counts, codes, code_norms, bank, bank_scale, loss_scale):
    width = m.shape[1]
    slope = 4.0 / math.sqrt(width)
    sharp = 1.0 / (width * contrast_temp)
    merged_scale = unit_scale(m)
    start = m * merged_scale
    residual = start
    trail = []
    for level in range(2):
        logits = dot3(residual, codes[level], NT) * slope - code_norms[level] * (0.5 * slope)
        probs = softmax(logits)
        chosen = dot3(probs, codes[level], NN)
        trail.append((residual, probs, chosen))
        residual = residual - chosen
    quantized = trail[0][2] + trail[1][2]
    anchor_scale = unit_scale(quantized)
    anchor = quantized * anchor_scale
    high, low = split(anchor)
    both = dot(jnp.concatenate([high, low], axis=0), bank, NT)
    used = counts > 0.0
    sims = jnp.where(used, (both[:8] + both[8:]) * bank_scale * sharp, -1e30)
    first = row_total(anchor * start) * sharp
    top = jnp.maximum(first, jnp.max(sims, axis=1, keepdims=True))
    first_exp = jnp.exp(first - top)
    bank_exp = counts * jnp.exp(sims - top)
    total = first_exp + row_total(bank_exp)
    recon = jnp.mean(residual * residual, axis=1, keepdims=True)
    loss = (top + jnp.log(total) - first + recon) * valid * loss_scale

    scale = valid * loss_scale
    first_grad = scale * (first_exp / total - 1.0) * sharp
    high, low = split(scale * bank_exp / total * bank_scale * sharp)
    both = dot(jnp.concatenate([high, low], axis=0), bank, NN)
    anchor_grad = first_grad * start + both[:8] + both[8:]
    start_grad = first_grad * anchor
    quant_grad = anchor_scale * (
        anchor_grad - anchor * jnp.mean(anchor * anchor_grad, axis=1, keepdims=True)
    )
    res_grad = residual * (scale * (2.0 / width))
    factors = [None, None]
    for level in (1, 0):
        before, probs, chosen = trail[level]
        chosen_grad = quant_grad - res_grad
        prob_grad = dot3(chosen_grad, codes[level], NT)
        logit_grad = probs * (prob_grad - row_total(probs * prob_grad)) * slope
        res_grad = res_grad + dot3(logit_grad, codes[level], NN)
        factors[level] = (probs, logit_grad, chosen_grad, before)
    start_grad = start_grad + res_grad
    merged_grad = merged_scale * (
        start_grad - start * jnp.mean(start * start_grad, axis=1, keepdims=True)
    )
    return loss, merged_grad, factors


def book_gradient(level, factor, books, bgrad):
    probs, logit_grad, chosen_grad, before = factor
    left_high, left_low = split(jnp.concatenate([probs, logit_grad], axis=0))
    right_high, right_low = split(jnp.concatenate([chosen_grad, before], axis=0))
    left = jnp.concatenate([left_high, left_high, left_low], axis=0)
    right = jnp.concatenate([right_high, right_low, right_high], axis=0)
    sums = dot(
        jnp.concatenate([left_high[8:], left_low[8:]], axis=0), jnp.ones((16, 256), BF), TN
    )
    for start in range(0, 1024, 256):
        at = slice(start, start + 256)
        bgrad[level, :, at] = dot(left, right[:, at], TN) - books[level, :, at] * sums


def train_body(
    pool, wcol, books, bank, cats_row, cats_col, cats_item, slot_col, neg,
    ugrad, bgrad, loss_ref,
    wv, act_buf, za, xo, xi, ms, ogs, rs_out, rs_in, gz, got, got2, jt, jz, jx, second, chigh, clow,
    w_sem, a_send, a_recv, m_send, m_recv, r_send, r_recv, u_send, u_recv,
    z1_send, z1_recv, q1_send, q1_recv, z2_send, z2_recv, q2_send, q2_recv, q3_send, q3_recv,
    zj_send, zj_recv, qj_send, qj_recv,
):
    seg, me = lax.axis_index("segment"), lax.axis_index("dp")
    z, q = me // NQ, me % NQ
    flip = 2 * (me % 2)
    block = seg ^ flip
    barrier = pltpu.get_barrier_semaphore()

    def seg_peer(step):
        return {"segment": lax.rem(seg + step, SEG)}

    def z_of(step):
        return lax.rem(z + step, NZ)

    def q_of(step):
        return lax.rem(q + step, NQ)

    def z_peer(step):
        return {"segment": seg, "dp": z_of(step) * NQ + q}

    def q_peer(step):
        return {"segment": block ^ (2 * (q_of(step) % 2)), "dp": z * NQ + q_of(step)}

    def remote(src, dst, send, recv, step, peer):
        return pltpu.make_async_remote_copy(
            src_ref=src,
            dst_ref=dst,
            send_sem=send.at[step],
            recv_sem=recv.at[step],
            device_id=peer,
            device_id_type=MESH,
        )

    def start_all(copies):
        for copy in copies:
            copy.start()

    def wait_all(copies):
        for copy in copies:
            copy.wait()

    for count, peer in ((SEG, seg_peer), (NZ, z_peer), (NQ, q_peer)):
        for step in range(1, count):
            pl.semaphore_signal(barrier, inc=1, device_id=peer(step), device_id_type=MESH)
    w_copy = pltpu.make_async_copy(wcol, wv, w_sem)
    w_copy.start()

    embedded = jnp.concatenate(
        [pool[0, :, 0:1024] + pool[1, :, 0:1024], pool[2] + pool[3]], axis=1
    )
    embedded = embedded.astype(BF).astype(F32)
    normed = (embedded * unit_scale(embedded)).astype(BF)
    w_copy.wait()
    hidden = dot(normed, wv[0:2560, :])
    bell = 0.5 * (1.0 + lax.erf(hidden * (1.0 / math.sqrt(2.0))))
    act_buf[block] = (hidden * bell).astype(BF)
    bell = bell + hidden * jnp.exp(-0.5 * hidden * hidden) * (1.0 / math.sqrt(2.0 * math.pi))
    pl.semaphore_wait(barrier, SEG + NZ + NQ - 3)
    a_copies = [
        remote(act_buf.at[block], act_buf.at[block], a_send, a_recv, step, seg_peer(step))
        for step in range(1, SEG)
    ]
    start_all(a_copies)

    lanes = iota((1, 512), 1)
    owner_e, place_e = slot_ids(
        cats_row[...], lanes // 128, lanes % 128, cats_col, slot_col[...]
    )
    item_dp = (lanes // 8 % 8) * 8 + lanes // 64
    item_row, item_key = lanes % 8 // 2, item_dp * 2 + lanes % 2
    owner_i, place_i = slot_ids(cats_item[...], item_row, item_key, cats_col, slot_col[...])
    select = iota((64, 512), 0) + z * 64 == owner_i * 8 + place_i
    fold = iota((512, 64), 0) == iota((512, 64), 1) + q * 64
    select = dot(
        jnp.where(select, 1.0, 0.0).astype(BF), jnp.where(fold, 1.0, 0.0).astype(BF)
    ).astype(BF)

    wait_all(a_copies)
    act = jnp.concatenate([act_buf[index] for index in range(SEG)], axis=1)
    merged = dot(act, wv[2560:3584, :])
    za[z] = jnp.concatenate([merged, bell], axis=0).astype(BF)
    z1_copies = [
        remote(za.at[z], za.at[z], z1_send, z1_recv, step, z_peer(step)) for step in range(1, NZ)
    ]
    start_all(z1_copies)

    joined = jnp.concatenate(
        [normed.astype(F32), act.astype(F32), jnp.zeros((8, 128), F32)], axis=1
    )
    for index in range(NDP):
        jt[index] = joined[:, index * 56 : index * 56 + 128].astype(BF)
    zj_copies = [
        remote(
            jt.at[pl.ds(pl.multiple_of(z_of(step) * NQ, NQ), NQ)],
            jz.at[z], zj_send, zj_recv, step, z_peer(step),
        )
        for step in range(1, NZ)
    ]
    start_all(zj_copies)
    jz[z] = jt[pl.ds(pl.multiple_of(z * NQ, NQ), NQ)]

    wait_all(z1_copies)
    arrived = za[...].astype(F32)
    xo[:, 0:8, :] = dot(select, arrived[:, 0:8].reshape(64, 256).astype(BF)).reshape(8, 8, 256).astype(BF)
    xo[:, 8:16, :] = dot(select, arrived[:, 8:16].reshape(64, 256).astype(BF)).reshape(8, 8, 256).astype(BF)
    q1_copies = [
        remote(xo.at[q_of(step)], xi.at[q], q1_send, q1_recv, step, q_peer(step))
        for step in range(1, NQ)
    ]
    start_all(q1_copies)
    xi[q] = xo[q]

    own = jnp.where(owner_e * 8 + place_e == iota((8, 512), 0) + me * 8, 1.0, 0.0)
    valid = row_total(own)
    picked = dot(neg[...].astype(F32).astype(BF), own.astype(BF), (((0,), (1,)), ((), ())))
    bins = iota((128, 256), 1).astype(F32)
    counts = jnp.concatenate(
        [
            jnp.sum(jnp.where(picked[:, k : k + 1] == bins, 1.0, 0.0), axis=0, keepdims=True)
            for k in range(8)
        ],
        axis=0,
    )
    ones = jnp.ones((8, 1024), BF)
    code_norms = []
    for level in range(2):
        for start in range(0, 256, 64):
            rows = slice(start, start + 64)
            high, low = split(books[level, rows, :])
            chigh[level, rows, :] = high
            clow[level, rows, :] = low
        high, low = split(books[level] * books[level])
        code_norms.append((dot(ones, high, NT) + dot(ones, low, NT))[0:1])
    wide = bank[...].astype(F32)
    high, low = split(wide * wide)
    bank_scale = lax.rsqrt(
        (dot(ones, high, NT) + dot(ones, low, NT))[0:1] * (1.0 / 1024.0) + norm_eps
    )

    wait_all(q1_copies)
    total = jnp.sum(xi[...].astype(F32), axis=0)
    bell = total[8:16]
    ms[block] = total[0:8].astype(BF)
    m_copies = [
        remote(ms.at[block], ms.at[block], m_send, m_recv, step, seg_peer(step))
        for step in range(1, SEG)
    ]
    start_all(m_copies)
    wait_all(zj_copies)
    qj_copies = [
        remote(jz.at[:, q_of(step)], jx.at[q], qj_send, qj_recv, step, q_peer(step))
        for step in range(1, NQ)
    ]
    start_all(qj_copies)
    jx[q] = jz[:, q]
    wait_all(m_copies)

    rows = jnp.concatenate([ms[index].astype(F32) for index in range(SEG)], axis=1)
    codes = [(chigh[level], clow[level]) for level in range(2)]
    loss, merged_grad, factors = quantize(
        rows, valid, counts, codes, code_norms, bank[...], bank_scale, 1.0 / math.sqrt(512.0)
    )
    loss_ref[...] = jnp.broadcast_to(jnp.sum(loss, axis=0, keepdims=True), (8, 128))
    out_grad = merged_grad.astype(BF)
    for index in range(SEG):
        ogs[index] = out_grad[:, index * 256 : (index + 1) * 256]
    partial = dot(ogs[block], wv[2560:3584, :], NT)
    for index in range(SEG):
        rs_out[index] = partial[:, index * 256 : (index + 1) * 256]
    r_copies = [
        remote(
            rs_out.at[lax.rem(seg + step, SEG) ^ flip], rs_in.at[block],
            r_send, r_recv, step, seg_peer(step),
        )
        for step in range(1, SEG)
    ]
    start_all(r_copies)
    rs_in[block] = rs_out[block]
    gz[1, z] = ogs[block]
    book_gradient(0, factors[0], books, bgrad)
    wait_all(r_copies)
    gz[0, z] = (jnp.sum(rs_in[...], axis=0) * bell).astype(BF)
    z2_copies = [
        remote(gz.at[:, z], gz.at[:, z], z2_send, z2_recv, step, z_peer(step))
        for step in range(1, NZ)
    ]
    start_all(z2_copies)
    book_gradient(1, factors[1], books, bgrad)
    wait_all(z2_copies)

    q2_copies = [
        remote(
            gz.at[(z * NQ + q_of(step)) // 46], got.at[q], q2_send, q2_recv, step, q_peer(step)
        )
        for step in range(1, NQ)
    ]
    start_all(q2_copies)
    q3_copies = [
        remote(gz.at[1], got2.at[q], q3_send, q3_recv, step, q_peer(step))
        for step in range(1, NQ)
    ]
    for step in range(1, NQ):

        @pl.when(z * NQ + q_of(step) == 45)
        def _(step=step):
            q3_copies[step - 1].start()

    got[q] = gz[me // 46]
    wait_all(qj_copies)
    columns = jx[...].astype(F32).reshape(512, 128).astype(BF)
    slots = iota((512, 512), 0) == (owner_i % 8) * 64 + (owner_i // 8) * 8 + place_i
    columns = dot(jnp.where(slots, 1.0, 0.0).astype(BF), columns).astype(BF)
    wait_all(q2_copies)
    grads = got[...].astype(F32).reshape(512, 256).astype(BF)
    second[...] = dot(columns, grads, TN)[0:56]

    @pl.when(me == 45)
    def _():
        got2[q] = gz[1]
        for copy in q3_copies:
            copy.wait_recv()
        others = dot(columns, got2[...].astype(F32).reshape(512, 256).astype(BF), TN)[0:56]
        second[...] = jnp.where(iota((56, 256), 0) < 2560 - 45 * 56, second[...], others)

    for step in range(1, NQ):

        @pl.when(z * NQ + q_of(step) == 45)
        def _(step=step):
            q3_copies[step - 1].wait_send()

    at = pl.ds(pl.multiple_of(block * 256, 256), 256)
    ugrad[:, at] = second[...]
    u_copies = [
        remote(ugrad.at[:, at], ugrad.at[:, at], u_send, u_recv, step, seg_peer(step))
        for step in range(1, SEG)
    ]
    start_all(u_copies)
    wait_all(u_copies)


def train(pool, wcol, books, bank, item_cats, cat_slot, neg_index):
    anywhere = pl.BlockSpec(memory_space=pl.ANY)
    vmem = pl.BlockSpec(memory_space=pltpu.VMEM)
    dma = pltpu.SemaphoreType.DMA
    cats = item_cats.reshape(512)
    by_item = item_cats.reshape(SEG, NZ, NQ, 2).transpose(2, 1, 0, 3)
    return pl.pallas_call(
        train_body,
        out_shape=(
            jax.ShapeDtypeStruct((56, 1024), F32),
            jax.ShapeDtypeStruct((2, 256, 1024), F32),
            jax.ShapeDtypeStruct((8, 128), F32),
        ),
        in_specs=[vmem, anywhere] + [vmem] * 7,
        out_specs=(vmem, vmem, vmem),
        scratch_shapes=[
            pltpu.VMEM((3584, 256), BF),
            pltpu.VMEM((SEG, 8, 256), BF),
            pltpu.VMEM((NZ, 16, 256), BF),
            pltpu.VMEM((NQ, 16, 256), BF),
            pltpu.VMEM((NQ, 16, 256), BF),
            pltpu.VMEM((SEG, 8, 256), BF),
            pltpu.VMEM((SEG, 8, 256), BF),
            pltpu.VMEM((SEG, 8, 256), F32),
            pltpu.VMEM((SEG, 8, 256), F32),
            pltpu.VMEM((2, NZ, 8, 256), BF),
            pltpu.VMEM((NQ, NZ, 8, 256), BF),
            pltpu.VMEM((NQ, NZ, 8, 256), BF),
            pltpu.VMEM((NDP, 8, 128), BF),
            pltpu.VMEM((NZ, NQ, 8, 128), BF),
            pltpu.VMEM((NQ, NZ, 8, 128), BF),
            pltpu.VMEM((56, 256), F32),
            pltpu.VMEM((2, 256, 1024), BF),
            pltpu.VMEM((2, 256, 1024), BF),
            dma,
        ]
        + [dma((SEG,))] * 8
        + [dma((8,))] * 14,
        compiler_params=pltpu.CompilerParams(
            collective_id=1, has_side_effects=True, vmem_limit_bytes=60 << 20
        ),
        name="train",
    )(
        pool,
        wcol.reshape(3584, 256),
        books.reshape(2, 256, 1024),
        bank.reshape(256, 1024),
        cats.reshape(1, 512),
        cats.reshape(512, 1),
        by_item.reshape(1, 512),
        cat_slot.astype(F32).reshape(NDP, 1),
        neg_index.reshape(512, 128),
    )


def per_device(
    images, texts, section_weights, uniting_weights, codebooks, neg_bank, item_cats, cat_slot, neg_index
):
    pool, wcol = encode(images, texts, section_weights, uniting_weights)
    ugrad, bgrad, loss = train(pool, wcol, codebooks, neg_bank, item_cats, cat_slot, neg_index)
    return ugrad, bgrad.reshape(codebooks.shape), loss[0:1, 0].reshape(1)


def solution(mesh):
    placed = (
        P("dp", None, None),
        P("dp", None, None),
        P("segment", None, None),
        P("dp", None),
        P("dp", None, None, None),
        P("dp", None, None),
        P(),
        P(),
        P(),
    )
    return jax.shard_map(
        per_device,
        mesh=mesh,
        in_specs=placed,
        out_specs=(P("dp", None), P("dp", None, None, None), P("dp")),
        check_vma=False,
    )
```

time: 953 us -> 117 us (0.12)
  blocking collectives: 742 us -> 0 us
  Pallas kernels: 0 us -> 105 us
  matrix products: 59.7 us -> 0 us
  waiting for transfers between devices: 53.9 us -> 0 us
  other arithmetic: 33.6 us -> 0.66 us
  local copies, waits for them, and re-layouts: 39.2 us -> 10.3 us
  between operations: 16.1 us -> 0.65 us
    all_gather x4 -> x0, blocking collectives: 612 us -> none  [the longest x1 160 us: per_device(): lax.all_gather(embedded, 'dp', axis=0, tiled=True)]
    psum x1 -> x0, blocking collectives: 117 us -> none  [per_device(): book_total, loss_owner = lax.psum((book_grad, loss_local), 'segment')]
    pallas_call x0 -> x2, Pallas kernels: none -> 105 us  [the longest x1 55.7 us: encode(): pl.pallas_call(encode_body, out_shape=(jax.ShapeDtypeStruct((SEG, 8, 1536...]
    psum x1 -> x0, waiting for transfers between devices: 53.2 us -> none  [per_device(): uniting_grad = lax.psum(segment_grad, 'segment')]
    dot_general x19 -> x0, matrix products: 49.1 us -> none  [the longest x1 9.95 us: image_attention(): jnp.einsum('bpd,de->bpe', normed, w_qkv, preferred_element_type=jnp.float32)]
    slice x9 -> x1, local copies, waits for them, and re-layouts: 23.5 us -> 1.18 us  [per_device(): return (ugrad, bgrad.reshape(codebooks.shape), loss[0:1, 0].reshape(1))]
    unnamed x1 -> x0, blocking collectives: 13.8 us -> none
    reduce_sum x18 -> x0, other arithmetic: 12.2 us -> none  [the longest x1 3.49 us: image_attention(): variance = jnp.mean(centred * centred, axis=-1, keepdims=True)]
  transfers between devices with their start and end apart: 2 -> 0, of which waited for: 1 -> 0; matrix products, arithmetic and copies ran while one was open for 8% -> 0% of each run, Pallas kernels for 0% -> 0%
where the time goes in v2:
time: 117 us
  Pallas kernels  105 us (90%)
  local copies, waits for them, and re-layouts  10.3 us (9%)
    pallas_call x1, Pallas kernels, encode(): pl.pallas_call(encode_body, out_shape=(jax.ShapeDtypeStruct((SEG, 8, 1536...  55.7 us
    pallas_call x1, Pallas kernels, train(): pl.pallas_call(train_body, out_shape=(jax.ShapeDtypeStruct((56, 1024), F3...  49.5 us
    unnamed x3, local copies, waits for them, and re-layouts  5.59 us

profile of v2, /device:TPU:1, one launch (start us, length us, event | category | flops | bytes accessed | tf_op | source)
XLA Modules:
  0.0 116.8 jit_solution(11003028573885322834)
XLA Ops:
  0.6 0.7 convert_bitcast_fusion
  1.3 0.7 copy.19.slot_col
  2.0 0.8 copy.16
  2.8 0.5 copy.17
  3.3 0.8 reshape.42.cats_item
  4.0 1.5 %copy.18.cats_col = s32[512,1]{1,0:T(8,128)} copy(s32[512,1]{0,1:T(1,128)} %bitcast.23) | data formatting | bytes 4096 | tf_op jit(solution)/shard_map/reshape;reshape | solution.py:691
  5.6 55.7 %encode.1 = (f32[4,8,1536]{2,1,0:T(8,128)}, bf16[64,56,256]{2,1,0:T(8,128)(2,1)}) custom-call(bf16[8,256,1024]{2,1,0:T(8,128)(2,1)} %images.1, bf16[512,1536]{1,0:T(8,128)(2,1)} %bitcast.19, bf16[21504,128]{1,0:T(8,128)(2,1)} %bitcast.15, bf16[56,1024]{1,0:T(8,128)(2,1)} %unit.1, f32[256,128]{1,0:T(8,128)} %constant.4.clone.cos_ref, ...), custom_call_target="tpu_custom_call" | custom-call | tf_op jit(solution)/shard_map/encode/pallas_call | solution.py:265
  61.3 49.5 %train.1 = (f32[56,1024]{1,0:T(8,128)}, f32[2,256,1024]{2,1,0:T(8,128)}, f32[8,128]{1,0:T(8,128)}) custom-call(f32[4,8,1536]{2,1,0:T(8,128)} %get-tuple-element.8.pool, bf16[3584,256]{1,0:T(8,128)(2,1)} %bitcast.18, f32[2,256,1024]{2,1,0:T(8,128)} %bitcast.16, bf16[256,1024]{1,0:T(8,128)(2,1)} %bitcast.20, s32[1,512]{1,0:T(1,128)} %bitcast.24, ...), custom_call_target="tpu_custom_call" | custom-call | tf_op jit(solution)/shard_map/train/pallas_call | solution.py:649
  110.8 1.2 %slice.3 = f32[1,1]{1,0:T(1,128)} slice(f32[8,128]{1,0:T(8,128)} %get-tuple-element.12), slice={[0:1], [0:1]} | slice | bytes 8 | tf_op jit(solution)/shard_map/slice | solution.py:703
  112.0 1.6 %copy.22 = f32[56,1024]{1,0:T(8,128)} copy(f32[56,1024]{1,0:T(8,128)} %get-tuple-element.16) | data formatting | bytes 458752
  113.6 3.2 %copy.23 = f32[1,2,256,1024]{3,2,1,0:T(8,128)} copy(f32[1,2,256,1024]{3,2,1,0:T(8,128)} %bitcast.17) | data formatting | bytes 4194304

commit v3 on v2

--- a/solution.py
+++ b/solution.py
@@ -18,6 +18,7 @@
 NZ = 8
 NQ = 8
 NDP = 64
+IMAGE_LEGS = (2, 5)
 
 norm_eps = 1e-06
 rope_theta = 1000000.0
@@ -80,13 +81,15 @@
     return jnp.sum(total, axis=0, keepdims=True)
 
 
-def image_part(flag, img, slot, stage, wi, wio, xn, qk, ysum, means, pool_row, img_sems, images):
+def image_part(flag, img, slot, stage, wi, wio, xn, qk, ysum, means, pool_row, img_sems, images, legs):
     relayout(slot, stage, 0, 1024, 12, wi)
     relayout(slot, stage, 12288, 512, 8, wio)
     lane = iota((1, 128), 1)
     masks = (lane < 64, lane >= 64)
 
     def item(index, carry):
+        for at, leg in zip(IMAGE_LEGS, legs):
+            pl.when(index == at)(leg)
         pltpu.make_async_copy(images.at[index], img.at[index], img_sems.at[index]).wait()
         total = None
         for start in range(0, 256, 32):
@@ -117,7 +120,7 @@
     pool_row[:, 1024:1536] = jnp.zeros((8, 512), F32)
 
 
-def text_part(flag, txt, slot, stage, wt, wto, xn, cos_ref, sin_ref, attended, means, pool_row):
+def text_part(flag, txt, slot, stage, wt, wto, xn, cos_ref, sin_ref, attended, means, pool_row, legs):
     relayout(slot, stage, 0, 1536, 8, wt)
     relayout(slot, stage, 12288, 768, 12, wto)
     attended[...] = jnp.zeros((8, 768), F32)
@@ -130,6 +133,8 @@
         return (tensor * cosine + pltpu.roll(tensor, 64, 1) * sine).astype(BF)
 
     def half(index, carry):
+        for at, leg in enumerate(legs):
+            pl.when(index == at)(leg)
         base = pl.multiple_of(index * 256, 256)
         for start in range(0, 256, 32):
             rows = txt[pl.ds(base + start, 32), :].astype(F32)
@@ -156,32 +161,44 @@
 
 def encode_body(
     images, texts, section, unit, cos_ref, sin_ref,
-    pool, wcol,
+    pool, wcol, wv,
     slot, stage, wi, wio, wt, wto, img, txt, xn, qk, ysum, means, attended, mine,
-    slot_sem, img_sems, txt_sem, own_sem, w_send, w_recv, s_send, s_recv,
+    slot_sem, img_sems, txt_sem, own_sem, w_sem, s_send, s_recv,
+    a_send, a_recv, b_send, b_recv, c_send, c_recv, d_send, d_recv, e_send, e_recv,
+    early,
 ):
     seg, me = lax.axis_index("segment"), lax.axis_index("dp")
     block = seg ^ (2 * (me % 2))
     is_image = seg < 2
     flag = jnp.where(seg % 2 == 0, 1.0, 0.0)
+    a_sems, b_sems, c_sems = (a_send, a_recv), (b_send, b_recv), (c_send, c_recv)
+    d_sems, e_sems = (d_send, d_recv), (e_send, e_recv)
     barrier = pltpu.get_barrier_semaphore()
-
-    def peer_of(step):
-        peer = lax.rem(me + step, NDP)
-        return {"segment": block ^ (2 * (peer % 2)), "dp": peer}
-
-    def greet(step, carry):
-        pl.semaphore_signal(barrier, inc=1, device_id=peer_of(step), device_id_type=MESH)
-        return carry
-
-    lax.fori_loop(1, NDP, greet, 0)
-    for step in range(1, SEG):
-        pl.semaphore_signal(
-            barrier, inc=1, device_id={"segment": lax.rem(seg + step, SEG)}, device_id_type=MESH
-        )
+    z, q = me // NQ, me % NQ
+
+    def z_at(step):
+        return lax.rem(z + step + NZ, NZ)
+
+    def q_at(step):
+        return lax.rem(q + step, NQ)
+
+    def z_peer(step):
+        return {"segment": seg, "dp": z_at(step) * NQ + q}
+
+    def q_peer(step):
+        return {"segment": block ^ (2 * (q_at(step) % 2)), "dp": z * NQ + q_at(step)}
+
+    def seg_peer(step):
+        return {"segment": lax.rem(seg + step, SEG)}
+
+    for count, peer in ((SEG, seg_peer), (NZ, z_peer), (NQ, q_peer)):
+        for step in range(1, count):
+            pl.semaphore_signal(barrier, inc=1, device_id=peer(step), device_id_type=MESH)
     slot_copy = pltpu.make_async_copy(section, slot, slot_sem)
     slot_copy.start()
     txt_copy = pltpu.make_async_copy(texts, txt, txt_sem)
+    for copy in early:
+        copy.start()
 
     @pl.when(is_image)
     def _():
@@ -196,37 +213,72 @@
         txt_copy.start()
 
     columns = pl.ds(pl.multiple_of(block * 256, 256), 256)
-    own = pltpu.make_async_copy(unit.at[:, columns], wcol.at[me], own_sem)
+    own = pltpu.make_async_copy(unit.at[:, columns], wcol.at[z, pl.ds(pl.multiple_of(q * 56, 8), 56)], own_sem)
     own.start()
-    pl.semaphore_wait(barrier, NDP - 1 + SEG - 1)
-
-    def w_copy(step):
+
+    left, right = slice(0, 128), slice(128, 256)
+    left_in = unit.at[:, pl.ds(pl.multiple_of(block * 256, 128), 128)]
+    right_in = unit.at[:, pl.ds(pl.multiple_of(block * 256 + 128, 128), 128)]
+
+    def remote(src, dst, pair, index, peer):
         return pltpu.make_async_remote_copy(
-            src_ref=unit.at[:, columns],
-            dst_ref=wcol.at[me],
-            send_sem=w_send.at[step],
-            recv_sem=w_recv.at[step],
-            device_id=peer_of(step),
+            src_ref=src,
+            dst_ref=dst,
+            send_sem=pair[0].at[index],
+            recv_sem=pair[1].at[index],
+            device_id=peer,
             device_id_type=MESH,
         )
 
-    def w_start(step, carry):
-        w_copy(step).start()
-        return carry
-
-    lax.fori_loop(1, NDP, w_start, 0)
+    def same(ref, pair, index, peer):
+        return remote(ref, ref, pair, index, peer)
+
+    first = [
+        remote(left_in, wcol.at[z, pl.ds(pl.multiple_of(q * 56, 8), 56), left], a_sems, step, q_peer(step)) for step in range(1, NQ)
+    ] + [
+        remote(right_in, wcol.at[z, pl.ds(pl.multiple_of(q * 56, 8), 56), right], b_sems, step, z_peer(step))
+        for step in range(1, NZ)
+    ]
+    middle = [
+        same(wcol.at[z, :, left], c_sems, index, z_peer(shift))
+        for index, shift in enumerate((1, -1, 2, -2))
+    ] + [same(wcol.at[:, pl.ds(pl.multiple_of(q * 56, 8), 56), right], d_sems, step, q_peer(step)) for step in range(1, NQ)]
+    last = [
+        same(wcol.at[z_at(-2), :, left], e_sems, 0, z_peer(1)),
+        same(wcol.at[z_at(2), :, left], e_sems, 1, z_peer(-1)),
+        same(wcol.at[z_at(-2), 0:224, left], e_sems, 2, z_peer(2)),
+        same(wcol.at[z_at(2), 224:448, left], e_sems, 3, z_peer(-2)),
+    ]
+
+    def second_leg():
+        own.wait()
+        for copy in first:
+            copy.wait()
+        for copy in middle:
+            copy.start()
+
+    def third_leg():
+        for copy in middle[2:4]:
+            copy.wait()
+        for copy in last:
+            copy.start()
+
+    pl.semaphore_wait(barrier, SEG + NZ + NQ - 3)
+    for copy in first:
+        copy.start()
     slot_copy.wait()
 
     @pl.when(is_image)
     def _():
         image_part(
-            flag, img, slot, stage, wi, wio, xn, qk, ysum, means, mine, img_sems, images
+            flag, img, slot, stage, wi, wio, xn, qk, ysum, means, mine, img_sems, images,
+            (second_leg, third_leg),
         )
 
     @pl.when(jnp.logical_not(is_image))
     def _():
         txt_copy.wait()
-        text_part(flag, txt, slot, stage, wt, wto, xn, cos_ref, sin_ref, attended, means, mine)
+        text_part(flag, txt, slot, stage, wt, wto, xn, cos_ref, sin_ref, attended, means, mine, (second_leg, third_leg))
 
     def pool_copy(step):
         return pltpu.make_async_remote_copy(
@@ -234,7 +286,7 @@
             dst_ref=pool.at[seg],
             send_sem=s_send.at[step],
             recv_sem=s_recv.at[step],
-            device_id={"segment": lax.rem(seg + step, SEG)},
+            device_id=seg_peer(step),
             device_id_type=MESH,
         )
 
@@ -242,63 +294,17 @@
         pool_copy(step).start()
     pool[seg] = mine[...]
 
-    def w_finish(step, carry):
-        w_copy(step).wait()
-        return carry
-
-    lax.fori_loop(1, NDP, w_finish, 0)
-    own.wait()
+    for copy in middle[:2] + middle[4:] + last:
+        copy.wait()
+    w_copies = [
+        pltpu.make_async_copy(wcol.at[index], wv.at[pl.ds(index * 448, 448)], w_sem.at[index])
+        for index in range(NZ)
+    ]
+    for copy in w_copies:
+        copy.start()
     for step in range(1, SEG):
         pool_copy(step).wait()
-
-
-def encode(images, texts, section, unit):
-    half = HEAD_TXT // 2
-    exponents = np.arange(half, dtype=np.float32) * np.float32(2.0 / HEAD_TXT)
-    inverse = np.exp(np.float32(-math.log(rope_theta)) * exponents).astype(np.float32)
-    angles = np.arange(64, dtype=np.float32)[:, None] * inverse[None, :]
-    cosine = np.tile(np.cos(angles), (4, 2)).astype(np.float32)
-    sine = np.tile(np.concatenate([-np.sin(angles), np.sin(angles)], axis=1), (4, 1))
-    anywhere = pl.BlockSpec(memory_space=pl.ANY)
-    vmem = pl.BlockSpec(memory_space=pltpu.VMEM)
-    dma = pltpu.SemaphoreType.DMA
-    return pl.pallas_call(
-        encode_body,
-        out_shape=(
-            jax.ShapeDtypeStruct((SEG, 8, 1536), F32),
-            jax.ShapeDtypeStruct((NDP, 56, 256), BF),
-        ),
-        in_specs=[anywhere, anywhere, anywhere, vmem, vmem, vmem],
-        out_specs=(vmem, anywhere),
-        scratch_shapes=[
-            pltpu.VMEM((21504, 128), BF),
-            pltpu.VMEM((768, 128), F32),
-            pltpu.VMEM((1024, 1536), BF),
-            pltpu.VMEM((512, 1024), BF),
-            pltpu.VMEM((1536, 1024), BF),
-            pltpu.VMEM((768, 1536), BF),
-            pltpu.VMEM((8, 256, 1024), BF),
-            pltpu.VMEM((512, 1536), BF),
-            pltpu.VMEM((256, 1536), BF),
-            pltpu.VMEM((256, 1024), BF),
-            pltpu.VMEM((64, 1024), F32),
-            pltpu.VMEM((8, 1536), F32),
-            pltpu.VMEM((8, 768), F32),
-            pltpu.VMEM((8, 1536), F32),
-            dma, dma((8,)), dma, dma, dma((NDP,)), dma((NDP,)), dma((SEG,)), dma((SEG,)),
-        ],
-        compiler_params=pltpu.CompilerParams(
-            collective_id=0, has_side_effects=True, vmem_limit_bytes=60 << 20
-        ),
-        name="encode",
-    )(
-        images,
-        texts.reshape(512, 1536),
-        section.reshape(21504, 128),
-        unit,
-        jnp.asarray(cosine, F32),
-        jnp.asarray(sine, F32),
-    )
+    return w_copies
 
 
 def softmax(logits):
@@ -310,20 +316,28 @@
     return jnp.sum(a, axis=1, keepdims=True)
 
 
-def slot_ids(cats, rows, keys, cats_col, slot_col):
-    named = iota((NDP, 512), 0) == cats
-    owner = jnp.sum(jnp.where(named, slot_col, 0.0), axis=0, keepdims=True)
-    rank = jnp.zeros((8, 512), F32)
-    for start in range(0, 512, 64):
-        entry = iota((64, 1), 0) + start
-        earlier = (
-            (cats_col[start : start + 64] == cats)
-            & (entry // 128 == rows)
-            & (entry % 128 < keys)
+def slot_tables(cats_ref, slot_ref):
+    cats = jnp.concatenate([cats_ref[...].astype(F32), jnp.zeros((4, 128), F32)], axis=0)
+    slots = jnp.broadcast_to(slot_ref[...].astype(F32), (8, NDP)).astype(BF)
+    square = iota((128, 128), 0), iota((128, 128), 1)
+    turned = dot(jnp.where(square[0] == square[1], 1.0, 0.0).astype(BF), cats.astype(BF), NT)
+    lanes = iota((1, 512), 1)
+    keys = ((lanes // 8 % 8) * 8 + lanes // 64) * 2 + lanes % 2
+    by_row, by_item = [], jnp.zeros((8, 512), F32)
+    for row in range(SEG):
+        named = cats[row : row + 1]
+        owner = dot(
+            slots, jnp.where(iota((NDP, 128), 0).astype(F32) == named, 1.0, 0.0).astype(BF)
         )
-        rank = rank + jnp.sum(jnp.where(earlier, 1.0, 0.0).reshape(8, 8, 512), axis=0)
-    rank = jnp.sum(rank, axis=0, keepdims=True)
-    return owner.astype(jnp.int32), rows * CAP + rank.astype(jnp.int32)
+        earlier = (turned[:, row : row + 1] == named) & (square[0] < square[1])
+        rank = jnp.sum(jnp.where(earlier, 1.0, 0.0), axis=0, keepdims=True)
+        place = row * CAP + rank
+        both = jnp.where(iota((8, 128), 0) == 0, owner, place)
+        by_row.append((owner[0:1] * 8.0 + place).astype(jnp.int32))
+        moved = (iota((128, 512), 0) == keys) & (lanes % 8 // 2 == row)
+        by_item = by_item + dot(both.astype(BF), jnp.where(moved, 1.0, 0.0).astype(BF))
+    by_item = by_item.astype(jnp.int32)
+    return jnp.concatenate(by_row, axis=1), by_item[0:1], by_item[1:2]
 
 
 def quantize(m, valid, counts, codes, code_norms, bank, bank_scale, loss_scale):
@@ -380,25 +394,58 @@
     return loss, merged_grad, factors
 
 
-def book_gradient(level, factor, books, bgrad):
+def book_factors(factor):
     probs, logit_grad, chosen_grad, before = factor
     left_high, left_low = split(jnp.concatenate([probs, logit_grad], axis=0))
     right_high, right_low = split(jnp.concatenate([chosen_grad, before], axis=0))
     left = jnp.concatenate([left_high, left_high, left_low], axis=0)
     right = jnp.concatenate([right_high, right_low, right_high], axis=0)
-    sums = dot(
-        jnp.concatenate([left_high[8:], left_low[8:]], axis=0), jnp.ones((16, 256), BF), TN
-    )
+    return left, right
+
+
+def finish_body(left, right, books, blocks, loss_in, ugrad, bgrad, loss):
+    rows = iota((48, 256), 0)
+    mask = jnp.where(((rows >= 8) & (rows < 16)) | (rows >= 40), 1.0, 0.0).astype(BF)
+    sums = dot(left[0], mask, TN)
     for start in range(0, 1024, 256):
         at = slice(start, start + 256)
-        bgrad[level, :, at] = dot(left, right[:, at], TN) - books[level, :, at] * sums
+        bgrad[0, :, at] = dot(left[0], right[0, :, at], TN) - books[0, :, at] * sums
+    for index in range(SEG):
+        ugrad[:, index * 256 : (index + 1) * 256] = blocks[index].astype(F32)
+    loss[0] = jnp.max(loss_in[...])
+
+
+def finish(left, right, books, blocks, loss):
+    smem = pl.BlockSpec(memory_space=pltpu.SMEM)
+    return pl.pallas_call(
+        finish_body,
+        grid=(2, 2),
+        out_shape=(
+            jax.ShapeDtypeStruct((56, 1024), F32),
+            jax.ShapeDtypeStruct((2, 256, 1024), F32),
+            jax.ShapeDtypeStruct((1,), F32),
+        ),
+        in_specs=[
+            pl.BlockSpec((1, 48, 128), lambda i, j: (i, 0, j)),
+            pl.BlockSpec((1, 48, 1024), lambda i, j: (i, 0, 0)),
+            pl.BlockSpec((1, 128, 1024), lambda i, j: (i, j, 0)),
+            pl.BlockSpec((SEG, 56, 256), lambda i, j: (0, 0, 0)),
+            pl.BlockSpec((8, 128), lambda i, j: (0, 0)),
+        ],
+        out_specs=(
+            pl.BlockSpec((56, 1024), lambda i, j: (0, 0)),
+            pl.BlockSpec((1, 128, 1024), lambda i, j: (i, j, 0)),
+            smem,
+        ),
+        name="finish",
+    )(left, right, books, blocks, loss)
 
 
 def train_body(
-    pool, wcol, books, bank, cats_row, cats_col, cats_item, slot_col, neg,
-    ugrad, bgrad, loss_ref,
-    wv, act_buf, za, xo, xi, ms, ogs, rs_out, rs_in, gz, got, got2, jt, jz, jx, second, chigh, clow,
-    w_sem, a_send, a_recv, m_send, m_recv, r_send, r_recv, u_send, u_recv,
+    pool, w_copies, books, bank, cats, slots, neg, book_copies, bank_copy, neg_copy,
+    blocks, left_ref, right_ref, loss_ref,
+    wv, act_buf, za, xo, xi, ms, ogs, r2, gz, got, got2, jt, jz, jx, second, chigh, clow,
+    own_sem, a_send, a_recv, m_send, m_recv, r_send, r_recv, u_send, u_recv,
     z1_send, z1_recv, q1_send, q1_recv, z2_send, z2_recv, q2_send, q2_recv, q3_send, q3_recv,
     zj_send, zj_recv, qj_send, qj_recv,
 ):
@@ -406,7 +453,6 @@
     z, q = me // NQ, me % NQ
     flip = 2 * (me % 2)
     block = seg ^ flip
-    barrier = pltpu.get_barrier_semaphore()
 
     def seg_peer(step):
         return {"segment": lax.rem(seg + step, SEG)}
@@ -441,36 +487,24 @@
         for copy in copies:
             copy.wait()
 
-    for count, peer in ((SEG, seg_peer), (NZ, z_peer), (NQ, q_peer)):
-        for step in range(1, count):
-            pl.semaphore_signal(barrier, inc=1, device_id=peer(step), device_id_type=MESH)
-    w_copy = pltpu.make_async_copy(wcol, wv, w_sem)
-    w_copy.start()
-
     embedded = jnp.concatenate(
         [pool[0, :, 0:1024] + pool[1, :, 0:1024], pool[2] + pool[3]], axis=1
     )
     embedded = embedded.astype(BF).astype(F32)
     normed = (embedded * unit_scale(embedded)).astype(BF)
-    w_copy.wait()
+    for copy in w_copies:
+        copy.wait()
     hidden = dot(normed, wv[0:2560, :])
     bell = 0.5 * (1.0 + lax.erf(hidden * (1.0 / math.sqrt(2.0))))
     act_buf[block] = (hidden * bell).astype(BF)
     bell = bell + hidden * jnp.exp(-0.5 * hidden * hidden) * (1.0 / math.sqrt(2.0 * math.pi))
-    pl.semaphore_wait(barrier, SEG + NZ + NQ - 3)
     a_copies = [
         remote(act_buf.at[block], act_buf.at[block], a_send, a_recv, step, seg_peer(step))
         for step in range(1, SEG)
     ]
     start_all(a_copies)
 
-    lanes = iota((1, 512), 1)
-    owner_e, place_e = slot_ids(
-        cats_row[...], lanes // 128, lanes % 128, cats_col, slot_col[...]
-    )
-    item_dp = (lanes // 8 % 8) * 8 + lanes // 64
-    item_row, item_key = lanes % 8 // 2, item_dp * 2 + lanes % 2
-    owner_i, place_i = slot_ids(cats_item[...], item_row, item_key, cats_col, slot_col[...])
+    by_entry, owner_i, place_i = slot_tables(cats, slots)
     select = iota((64, 512), 0) + z * 64 == owner_i * 8 + place_i
     fold = iota((512, 64), 0) == iota((512, 64), 1) + q * 64
     select = dot(
@@ -485,6 +519,20 @@
         remote(za.at[z], za.at[z], z1_send, z1_recv, step, z_peer(step)) for step in range(1, NZ)
     ]
     start_all(z1_copies)
+
+    def w2_rows(index):
+        return wv.at[pl.ds(pl.multiple_of(2560 + index * 256, 256), 256)]
+
+    r_copies = [
+        remote(
+            w2_rows(lax.rem(seg + step, SEG) ^ flip), r2.at[block],
+            r_send, r_recv, step, seg_peer(step),
+        )
+        for step in range(1, SEG)
+    ]
+    start_all(r_copies)
+    own_rows = pltpu.make_async_copy(w2_rows(block), r2.at[block], own_sem)
+    own_rows.start()
 
     joined = jnp.concatenate(
         [normed.astype(F32), act.astype(F32), jnp.zeros((8, 128), F32)], axis=1
@@ -512,7 +560,11 @@
     start_all(q1_copies)
     xi[q] = xo[q]
 
-    own = jnp.where(owner_e * 8 + place_e == iota((8, 512), 0) + me * 8, 1.0, 0.0)
+    neg_copy.wait()
+    bank_copy.wait()
+    for copy in book_copies:
+        copy.wait()
+    own = jnp.where(by_entry == iota((8, 512), 0) + me * 8, 1.0, 0.0)
     valid = row_total(own)
     picked = dot(neg[...].astype(F32).astype(BF), own.astype(BF), (((0,), (1,)), ((), ())))
     bins = iota((128, 256), 1).astype(F32)
@@ -566,28 +618,20 @@
     out_grad = merged_grad.astype(BF)
     for index in range(SEG):
         ogs[index] = out_grad[:, index * 256 : (index + 1) * 256]
-    partial = dot(ogs[block], wv[2560:3584, :], NT)
-    for index in range(SEG):
-        rs_out[index] = partial[:, index * 256 : (index + 1) * 256]
-    r_copies = [
-        remote(
-            rs_out.at[lax.rem(seg + step, SEG) ^ flip], rs_in.at[block],
-            r_send, r_recv, step, seg_peer(step),
-        )
-        for step in range(1, SEG)
-    ]
-    start_all(r_copies)
-    rs_in[block] = rs_out[block]
+    own_rows.wait()
+    wait_all(r_copies)
+    act_grad = dot(ogs[0], r2[0], NT)
+    for index in range(1, SEG):
+        act_grad = act_grad + dot(ogs[index], r2[index], NT)
     gz[1, z] = ogs[block]
-    book_gradient(0, factors[0], books, bgrad)
-    wait_all(r_copies)
-    gz[0, z] = (jnp.sum(rs_in[...], axis=0) * bell).astype(BF)
+    gz[0, z] = (act_grad * bell).astype(BF)
     z2_copies = [
         remote(gz.at[:, z], gz.at[:, z], z2_send, z2_recv, step, z_peer(step))
         for step in range(1, NZ)
     ]
     start_all(z2_copies)
-    book_gradient(1, factors[1], books, bgrad)
+    for level in range(2):
+        left_ref[level], right_ref[level] = book_factors(factors[level])
     wait_all(z2_copies)
 
     q2_copies = [
@@ -630,77 +674,144 @@
         def _(step=step):
             q3_copies[step - 1].wait_send()
 
-    at = pl.ds(pl.multiple_of(block * 256, 256), 256)
-    ugrad[:, at] = second[...]
+    blocks[block] = second[...].astype(BF)
     u_copies = [
-        remote(ugrad.at[:, at], ugrad.at[:, at], u_send, u_recv, step, seg_peer(step))
+        remote(blocks.at[block], blocks.at[block], u_send, u_recv, step, seg_peer(step))
         for step in range(1, SEG)
     ]
     start_all(u_copies)
     wait_all(u_copies)
 
 
-def train(pool, wcol, books, bank, item_cats, cat_slot, neg_index):
+ENCODE_VMEM = (
+    ((SEG, 8, 1536), F32),
+    ((3584, 256), BF),
+    ((21504, 128), BF),
+    ((768, 128), F32),
+    ((1024, 1536), BF),
+    ((512, 1024), BF),
+    ((1536, 1024), BF),
+    ((768, 1536), BF),
+    ((8, 256, 1024), BF),
+    ((512, 1536), BF),
+    ((256, 1536), BF),
+    ((256, 1024), BF),
+    ((64, 1024), F32),
+    ((8, 1536), F32),
+    ((8, 768), F32),
+    ((8, 1536), F32),
+)
+ENCODE_SEMS = (0, 8, 0, 0, 8, SEG, SEG, 8, 8, 8, 8, 4, 4, 8, 8, 4, 4)
+TRAIN_VMEM = (
+    ((SEG, 8, 256), BF),
+    ((NZ, 16, 256), BF),
+    ((NQ, 16, 256), BF),
+    ((NQ, 16, 256), BF),
+    ((SEG, 8, 256), BF),
+    ((SEG, 8, 256), BF),
+    ((SEG, 256, 256), BF),
+    ((2, NZ, 8, 256), BF),
+    ((NQ, NZ, 8, 256), BF),
+    ((NQ, NZ, 8, 256), BF),
+    ((NDP, 8, 128), BF),
+    ((NZ, NQ, 8, 128), BF),
+    ((NQ, NZ, 8, 128), BF),
+    ((56, 256), F32),
+    ((2, 256, 1024), BF),
+    ((2, 256, 1024), BF),
+)
+TRAIN_SEMS = (0,) + (SEG,) * 8 + (8,) * 14
+LOAD_VMEM = (((2, 256, 1024), F32), ((256, 1024), BF), ((512, 128), jnp.int32))
+LOAD_SEMS = (2, 0, 0)
+
+
+def whole_body(*refs):
+    images, texts, section, unit, cosine, sine, books, bank, cats, slots, neg = refs[:11]
+    wcol, blocks, left, right, loss = refs[11:16]
+    groups, at = [], 16
+    for part in (ENCODE_VMEM, TRAIN_VMEM, LOAD_VMEM, ENCODE_SEMS, TRAIN_SEMS, LOAD_SEMS):
+        groups.append(refs[at : at + len(part)])
+        at += len(part)
+    encode_vmem, train_vmem, load_vmem, encode_sems, train_sems, load_sems = groups
+    pool, wv = encode_vmem[:2]
+    books_v, bank_v, neg_v = load_vmem
+    book_copies = [
+        pltpu.make_async_copy(books.at[level], books_v.at[level], load_sems[0].at[level])
+        for level in range(2)
+    ]
+    bank_copy = pltpu.make_async_copy(bank, bank_v, load_sems[1])
+    neg_copy = pltpu.make_async_copy(neg, neg_v, load_sems[2])
+    w_copies = encode_body(
+        images, texts, section, unit, cosine, sine, pool, wcol, wv, *encode_vmem[2:], *encode_sems,
+        [*book_copies, bank_copy, neg_copy],
+    )
+    train_body(
+        pool, w_copies, books_v, bank_v, cats, slots, neg_v, book_copies, bank_copy, neg_copy,
+        blocks, left, right, loss, wv, *train_vmem, *train_sems,
+    )
+
+
+def whole(images, texts, section, unit, books, bank, cats, slots, neg):
+    half = HEAD_TXT // 2
+    exponents = np.arange(half, dtype=np.float32) * np.float32(2.0 / HEAD_TXT)
+    inverse = np.exp(np.float32(-math.log(rope_theta)) * exponents).astype(np.float32)
+    angles = np.arange(64, dtype=np.float32)[:, None] * inverse[None, :]
+    cosine = np.tile(np.cos(angles), (4, 2)).astype(np.float32)
+    sine = np.tile(np.concatenate([-np.sin(angles), np.sin(angles)], axis=1), (4, 1))
     anywhere = pl.BlockSpec(memory_space=pl.ANY)
     vmem = pl.BlockSpec(memory_space=pltpu.VMEM)
     dma = pltpu.SemaphoreType.DMA
-    cats = item_cats.reshape(512)
-    by_item = item_cats.reshape(SEG, NZ, NQ, 2).transpose(2, 1, 0, 3)
+    buffers = ENCODE_VMEM + TRAIN_VMEM + LOAD_VMEM
+    semaphores = ENCODE_SEMS + TRAIN_SEMS + LOAD_SEMS
     return pl.pallas_call(
-        train_body,
+        whole_body,
         out_shape=(
-            jax.ShapeDtypeStruct((56, 1024), F32),
-            jax.ShapeDtypeStruct((2, 256, 1024), F32),
+            jax.ShapeDtypeStruct((NZ, NQ * 56, 256), BF),
+            jax.ShapeDtypeStruct((SEG, 56, 256), BF),
+            jax.ShapeDtypeStruct((2, 48, 256), BF),
+            jax.ShapeDtypeStruct((2, 48, 1024), BF),
             jax.ShapeDtypeStruct((8, 128), F32),
         ),
-        in_specs=[vmem, anywhere] + [vmem] * 7,
-        out_specs=(vmem, vmem, vmem),
-        scratch_shapes=[
-            pltpu.VMEM((3584, 256), BF),
-            pltpu.VMEM((SEG, 8, 256), BF),
-            pltpu.VMEM((NZ, 16, 256), BF),
-            pltpu.VMEM((NQ, 16, 256), BF),
-            pltpu.VMEM((NQ, 16, 256), BF),
-            pltpu.VMEM((SEG, 8, 256), BF),
-            pltpu.VMEM((SEG, 8, 256), BF),
-            pltpu.VMEM((SEG, 8, 256), F32),
-            pltpu.VMEM((SEG, 8, 256), F32),
-            pltpu.VMEM((2, NZ, 8, 256), BF),
-            pltpu.VMEM((NQ, NZ, 8, 256), BF),
-            pltpu.VMEM((NQ, NZ, 8, 256), BF),
-            pltpu.VMEM((NDP, 8, 128), BF),
-            pltpu.VMEM((NZ, NQ, 8, 128), BF),
-            pltpu.VMEM((NQ, NZ, 8, 128), BF),
-            pltpu.VMEM((56, 256), F32),
-            pltpu.VMEM((2, 256, 1024), BF),
-            pltpu.VMEM((2, 256, 1024), BF),
-            dma,
-        ]
-        + [dma((SEG,))] * 8
-        + [dma((8,))] * 14,
+        in_specs=[anywhere] * 3 + [vmem] * 3 + [anywhere] * 2 + [vmem] * 2 + [anywhere],
+        out_specs=(anywhere, vmem, vmem, vmem, vmem),
+        scratch_shapes=[pltpu.VMEM(*buffer) for buffer in buffers]
+        + [dma((count,)) if count else dma for count in semaphores],
         compiler_params=pltpu.CompilerParams(
-            collective_id=1, has_side_effects=True, vmem_limit_bytes=60 << 20
+            collective_id=0, has_side_effects=True, vmem_limit_bytes=60 << 20
         ),
-        name="train",
+        name="whole",
     )(
-        pool,
-        wcol.reshape(3584, 256),
-        books.reshape(2, 256, 1024),
-        bank.reshape(256, 1024),
-        cats.reshape(1, 512),
-        cats.reshape(512, 1),
-        by_item.reshape(1, 512),
-        cat_slot.astype(F32).reshape(NDP, 1),
-        neg_index.reshape(512, 128),
+        images,
+        texts.reshape(512, 1536),
+        section.reshape(21504, 128),
+        unit,
+        jnp.asarray(cosine, F32),
+        jnp.asarray(sine, F32),
+        books,
+        bank,
+        cats,
+        slots,
+        neg,
     )
 
 
 def per_device(
     images, texts, section_weights, uniting_weights, codebooks, neg_bank, item_cats, cat_slot, neg_index
 ):
-    pool, wcol = encode(images, texts, section_weights, uniting_weights)
-    ugrad, bgrad, loss = train(pool, wcol, codebooks, neg_bank, item_cats, cat_slot, neg_index)
-    return ugrad, bgrad.reshape(codebooks.shape), loss[0:1, 0].reshape(1)
+    books = codebooks.reshape(2, 256, 1024)
+    _, blocks, left, right, loss = whole(
+        images,
+        texts,
+        section_weights,
+        uniting_weights,
+        books,
+        neg_bank.reshape(256, 1024),
+        item_cats.reshape(SEG, 128),
+        cat_slot.reshape(1, NDP),
+        neg_index.reshape(512, 128),
+    )
+    ugrad, bgrad, loss = finish(left, right, books, blocks, loss)
+    return ugrad, bgrad.reshape(codebooks.shape), loss
 
 
 def solution(mesh):

time: 117 us -> 79.2 us (0.68)
  Pallas kernels: 105 us -> 78.3 us
  local copies, waits for them, and re-layouts: 10.3 us -> 0 us
    pallas_call x2, Pallas kernels: 105 us -> 78.3 us  [the longest x1 73.9 us: whole(): pl.pallas_call(whole_body, out_shape=(jax.ShapeDtypeStruct((NZ, NQ * 56,...]
    unnamed x3 -> x0, local copies, waits for them, and re-layouts: 5.59 us -> none
    another operation x1 -> x0, local copies, waits for them, and re-layouts: 1.53 us -> none  [train(): cats.reshape(512, 1)]
    reshape x2 -> x0, local copies, waits for them, and re-layouts: 1.47 us -> none  [the longest x1 0.75 us: train(): by_item.reshape(1, 512)]
    slice x1 -> x0, local copies, waits for them, and re-layouts: 1.18 us -> none  [per_device(): return (ugrad, bgrad.reshape(codebooks.shape), loss[0:1, 0].reshape(1))]
where the time goes in v3:
time: 79.2 us; the launch traced here: 79 us
  Pallas kernels  78.3 us (99%)
    pallas_call x1, Pallas kernels, whole(): pl.pallas_call(whole_body, out_shape=(jax.ShapeDtypeStruct((NZ, NQ * 56,...  73.9 us
    pallas_call x1, Pallas kernels, finish(): pl.pallas_call(finish_body, grid=(2, 2), out_shape=(jax.ShapeDtypeStruct(...  4.42 us

profile of v3, /device:TPU:1, one launch (start us, length us, event | category | flops | bytes accessed | tf_op | source)
XLA Modules:
  0.0 79.0 jit_solution(5878846355174120815)
XLA Ops:
  0.6 73.9 %whole.1 = (bf16[8,448,256]{2,1,0:T(8,128)(2,1)}, bf16[4,56,256]{2,1,0:T(8,128)(2,1)}, bf16[2,48,256]{2,1,0:T(8,128)(2,1)}, bf16[2,48,1024]{2,1,0:T(8,128)(2,1)}, f32[8,128]{1,0:T(8,128)}) custom-call(bf16[8,256,1024]{2,1,0:T(8,128)(2,1)} %refs_0_.1, bf16[512,1536]{1,0:T(8,128)(2,1)} %bitcast.11, bf16[21504,128]{1,0:T(8,128)(2,1)} %bitcast.10, ...), custom_call_target="tpu_custom_call" | custom-call | tf_op jit(solution)/shard_map/whole/pallas_call | solution.py:766
  74.6 4.4 %finish.1 = (f32[56,1024]{1,0:T(8,128)}, f32[2,256,1024]{2,1,0:T(8,128)}, f32[1]{0:T(128)}) custom-call(bf16[2,48,256]{2,1,0:T(8,128)(2,1)} %get-tuple-element.10.left, bf16[2,48,1024]{2,1,0:T(8,128)(2,1)} %get-tuple-element.11.right, f32[2,256,1024]{2,1,0:T(8,128)} %bitcast.9, bf16[4,56,256]{2,1,0:T(8,128)(2,1)} %get-tuple-element.12.blocks, ...), custom_call_target="tpu_custom_call" | custom-call | tf_op jit(solution)/shard_map/finish/pallas_call | solution.py:420
